TPU v7x, 128 devices: a whole 4x4x4 slice. The times are simulated.
128 devices in a mesh: trk: 16 (over z, y), mod: 8 (over x, core).
Axes of the slice: x: 4, y: 4, z: 4, core: 2. Of those that a mesh axis runs over, the one named last changes fastest.
Arguments:
- local_deriv: float32 [5, 12, 65536], P(None, None, ('trk', 'mod')), may hold values from -6 to 6
- global_deriv: float32 [8, 12, 65536], P(None, None, ('trk', 'mod')), may hold values from -6 to 6
- measured: float32 [12, 65536], P(None, ('trk', 'mod')), may hold values from -5 to 5
- hit_weight: float32 [12, 65536], P(None, ('trk', 'mod')), may hold values from 0.25 to 4
- hit_module: int32 [12, 65536], P(None, ('trk', 'mod')), may hold values from 0 to 65535, as said below
- hit_count: int32 [65536], P(('trk', 'mod')), may hold values from 6 to 12
- track_road: int32 [65536], P(('trk', 'mod')), may hold values from 0 to 8191, as said below
- road_start: int32 [8192], P(('trk', 'mod')), may hold values from 0 to 65535, as said below
- prior_weight: float32 [65536, 8], P(('trk', 'mod')), may hold values from 0.5 to 8
Outputs:
- normal_blocks: float32 [8192, 128, 128], P(('trk', 'mod'))
- rhs: float32 [65536, 8], P(('trk', 'mod'))
- corrections: float32 [65536, 8], P(('trk', 'mod'))
Inputs may be any that keep to these rules, and one draw needn't show every extreme that they name: `hit_module`: each hit slot of track t, padding too, names one of the 16 modules (road_start[track_road[t]] + k) mod 65536, k = 0 to 15; the slots of one track name different modules. `track_road`: call the device that holds road_start[r] the owner of road r. At most 16 of the 512 tracks of one device belong to roads of one owner; one owner receives exactly 16 tracks from every device. road_start[r] lies between 16 / 2 * r and 16 / 2 * r + 16 / 2 - 1.
All inputs are finite; a program needn't handle non-finite values.
Results may differ from a plain program's by a relative error of at most 0.00016.
Values sent between devices are 32-bit elements; how exact they have to be, the bound alone decides.
A program may use at most 128 MiB of HBM per device.

v0:
```python
import jax
import jax.numpy as jnp
from jax import lax
from jax.sharding import PartitionSpec as P

NPAR = 8
NHIT = 12
ROAD = 16
NMOD = 65536


EPS = 1e-06
HIGHEST = lax.Precision.HIGHEST


def from_behind(value, axis, steps):
    count = lax.axis_size(axis)
    pairs = [(source, (source + steps) % count) for source in range(count)]
    return lax.ppermute(value, axis, pairs)


def local_fit(local_deriv, measured, hit_weight, hit_count):
    nlocal = local_deriv.shape[0]
    hit_slots = local_deriv.shape[1]
    position = lax.broadcasted_iota(jnp.int32, hit_weight.shape, 0)
    weight = jnp.where(position < hit_count[None, :], hit_weight, jnp.zeros_like(hit_weight))
    weighted = local_deriv * weight[None]
    local_gram = jnp.sum(weighted[:, None] * local_deriv[None, :], axis=2)
    factor = {}
    for row_num in range(nlocal):
        for col_num in range(row_num + 1):
            running = local_gram[row_num, col_num]
            if row_num == col_num:
                running = running + 1.0
            for inner_num in range(col_num):
                running = running - factor[row_num, inner_num] * factor[col_num, inner_num]
            if row_num == col_num:
                factor[row_num, col_num] = jnp.sqrt(running)
            else:
                factor[row_num, col_num] = running / factor[col_num, col_num]
    solved_rows = []
    for row_num in range(nlocal):
        running = weighted[row_num]
        for col_num in range(row_num):
            running = running - factor[row_num, col_num][None] * solved_rows[col_num]
        solved_rows.append(running / factor[row_num, row_num][None])
    projected = jnp.stack(solved_rows)
    diagonal = jnp.eye(hit_slots, dtype=jnp.float32)[:, :, None] * weight[None]
    schur_block = diagonal - jnp.sum(projected[:, :, None] * projected[:, None, :], axis=0)
    solved = jnp.sum(schur_block * measured[None], axis=1)
    return (schur_block, solved, projected, weight)


def minres_finish(beta_one, alpha_one, beta_two, alpha_two, beta_three, lanczos_one, lanczos_two):
    entry_first = alpha_one * alpha_one + beta_two * beta_two
    entry_cross = beta_two * (alpha_one + alpha_two)
    entry_second = beta_two * beta_two + alpha_two * alpha_two + beta_three * beta_three
    determinant = entry_first * entry_second - entry_cross * entry_cross
    coef_one = beta_one * (entry_second * alpha_one - entry_cross * beta_two) / determinant
    coef_two = beta_one * (entry_first * beta_two - entry_cross * alpha_one) / determinant
    return coef_one * lanczos_one + coef_two * lanczos_two


def global_sum(local_term):
    return lax.psum(local_term, ("trk", "mod"))


def lanczos_pair(direction, mapped):
    alpha_val = global_sum(jnp.sum(direction * mapped))
    residue = mapped - alpha_val * direction
    beta_val = jnp.sqrt(global_sum(jnp.sum(residue * residue)) + EPS)
    return (alpha_val, beta_val, residue)


def fold_rim(extended, owned_rows):
    returned = from_behind(extended[owned_rows:], ("trk", "mod"), 1)
    return extended[:owned_rows].at[: returned.shape[0]].add(returned)


def on_device(
    local_deriv,
    global_deriv,
    measured,
    hit_weight,
    hit_module,
    hit_count,
    track_road,
    road_start,
    prior_weight,
):
    devices = lax.axis_size(("trk", "mod"))
    road_dev = road_start.shape[0]
    owned_rows = prior_weight.shape[0]
    tracks_here = hit_count.shape[0]
    capacity = 4 * tracks_here // devices
    slots_all = devices * capacity
    schur_block, solved, projected, weight = local_fit(local_deriv, measured, hit_weight, hit_count)
    global_rows = jnp.transpose(global_deriv, (2, 1, 0)).reshape(tracks_here, NHIT * NPAR)
    payload = jnp.concatenate(
        [
            global_rows,
            jnp.transpose(schur_block, (2, 0, 1)).reshape(tracks_here, NHIT * NHIT),
            solved.T,
        ],
        axis=1,
    )
    width_all = payload.shape[1]
    owner_dev = track_road // road_dev
    member = (
        owner_dev[:, None] == lax.broadcasted_iota(jnp.int32, (tracks_here, devices), 1)
    ).astype(jnp.int32)
    rank_in = jnp.sum(jnp.cumsum(member, axis=0) * member, axis=1) - 1
    target = owner_dev * capacity + rank_in
    send_values = jnp.zeros((slots_all, width_all), jnp.float32).at[target].set(payload)
    send_modules = jnp.zeros((slots_all, NHIT), jnp.int32).at[target].set(hit_module.T)
    send_roads = jnp.zeros((slots_all,), jnp.int32).at[target].set(track_road % road_dev)
    recv_values, recv_modules, recv_roads = (
        lax.all_to_all(send_values, ("trk", "mod"), split_axis=0, concat_axis=0, tiled=True),
        lax.all_to_all(send_modules, ("trk", "mod"), split_axis=0, concat_axis=0, tiled=True),
        lax.all_to_all(send_roads, ("trk", "mod"), split_axis=0, concat_axis=0, tiled=True),
    )
    columns_global = NHIT * NPAR
    recv_global = recv_values[:, :columns_global].reshape(slots_all, NHIT, NPAR)
    recv_solved = recv_values[:, width_all - NHIT :]
    recv_schur = recv_values[:, columns_global : columns_global + NHIT * NHIT].reshape(
        slots_all, NHIT, NHIT
    )
    road_match = (
        recv_roads[:, None] == lax.broadcasted_iota(jnp.int32, (slots_all, road_dev), 1)
    ).astype(jnp.int32)
    road_hot = road_match.astype(jnp.float32)
    start_of = jnp.sum(road_match * road_start[None, :], axis=1)
    slot_num = jnp.clip((recv_modules - start_of[:, None]) % NMOD, 0, ROAD - 1)
    slot_hot = (
        slot_num[:, :, None] == lax.broadcasted_iota(jnp.int32, (slots_all, NHIT, ROAD), 2)
    ).astype(jnp.float32)
    laid = (slot_hot[:, :, :, None] * recv_global[:, :, None, :]).reshape(
        slots_all, NHIT, ROAD * NPAR
    )
    block_count = 8
    rows_each = slots_all // block_count
    block_width = ROAD * NPAR

    def accumulate(total, pieces):
        part_laid, part_schur, part_road = pieces
        outer = jnp.zeros((rows_each, block_width, block_width), jnp.float32)
        for row_num in range(NHIT):
            mixed_row = jnp.zeros((rows_each, block_width), jnp.float32)
            for col_num in range(NHIT):
                mixed_row = (
                    mixed_row + part_schur[:, row_num, col_num][:, None] * part_laid[:, col_num]
                )
            outer = outer + part_laid[:, row_num][:, :, None] * mixed_row[:, None, :]
        flat_outer = outer.reshape(rows_each, block_width * block_width)
        return (
            total
            + jnp.dot(
                part_road.T, flat_outer, precision=HIGHEST, preferred_element_type=jnp.float32
            ),
            None,
        )

    start_total = jnp.zeros((road_dev, block_width * block_width), jnp.float32)
    total, unused = lax.scan(
        accumulate,
        start_total,
        (
            laid.reshape(block_count, rows_each, NHIT, block_width),
            recv_schur.reshape(block_count, rows_each, NHIT, NHIT),
            road_hot.reshape(block_count, rows_each, road_dev),
        ),
    )
    normal_blocks = total.reshape(road_dev, block_width, block_width)
    spacing = ROAD // 2
    local_start = spacing * lax.broadcasted_iota(jnp.int32, (road_dev,), 0) + road_start % spacing
    gather_index = local_start[:, None] + lax.broadcasted_iota(jnp.int32, (road_dev, ROAD), 1)
    track_rhs = jnp.sum(laid * recv_solved[:, :, None], axis=1)
    road_rhs = jnp.dot(road_hot.T, track_rhs, precision=HIGHEST, preferred_element_type=jnp.float32)
    extended = (
        jnp.zeros((owned_rows + ROAD, NPAR), jnp.float32)
        .at[gather_index.reshape(-1)]
        .add(road_rhs.reshape(-1, NPAR))
    )
    rhs = fold_rim(extended, owned_rows)

    def apply_normal(vector):
        rim_rows = from_behind(vector[:ROAD], ("trk", "mod"), -1)
        extended_vec = jnp.concatenate([vector, rim_rows], axis=0)
        pieces = extended_vec[gather_index].reshape(road_dev, ROAD * NPAR)
        mapped = jnp.sum(normal_blocks * pieces[:, None, :], axis=2)
        spread = (
            jnp.zeros_like(extended_vec).at[gather_index.reshape(-1)].add(mapped.reshape(-1, NPAR))
        )
        return prior_weight * vector + fold_rim(spread, owned_rows)

    beta_one = jnp.sqrt(global_sum(jnp.sum(rhs * rhs)) + EPS)
    lanczos_one = rhs / beta_one
    alpha_one, beta_two, residue = lanczos_pair(lanczos_one, apply_normal(lanczos_one))
    lanczos_two = residue / beta_two
    alpha_two, beta_three, residue = lanczos_pair(
        lanczos_two, apply_normal(lanczos_two) - beta_two * lanczos_one
    )
    corrections = minres_finish(
        beta_one, alpha_one, beta_two, alpha_two, beta_three, lanczos_one, lanczos_two
    )
    return (normal_blocks, rhs, corrections)


def solution(mesh):
    in_specs = (
        P(None, None, ("trk", "mod")),
        P(None, None, ("trk", "mod")),
        P(None, ("trk", "mod")),
        P(None, ("trk", "mod")),
        P(None, ("trk", "mod")),
        P(("trk", "mod")),
        P(("trk", "mod")),
        P(("trk", "mod")),
        P(("trk", "mod"), None),
    )
    out_specs = (P(("trk", "mod"), None, None), P(("trk", "mod"), None), P(("trk", "mod"), None))
    return jax.shard_map(
        on_device, mesh=mesh, in_specs=in_specs, out_specs=out_specs, check_vma=False
    )
```

profile of v0, /device:TPU:1, one launch (start us, length us, event | category | flops | bytes accessed | tf_op | source)
XLA Modules:
  0.0 1322.1 jit_solution(3779098838380929699)
XLA Ops:
  2.0 2.5 scatter_custom_fusion
  5.2 11.5 all-to-all-start
  26.2 9.6 all-to-all-start.1
  37.1 3.6 scatter_custom_fusion.2
  40.7 5.2 all-to-all-done.1
  45.9 5.2 all-to-all-start.2
  59.7 21.7 %all-to-all-done.2 = f32[128,16,252]{2,1,0:T(8,128)S(1)} async-done(((f32[128,16,252]{2,1,0:T(8,128)}), f32[128,16,252]{2,1,0:T(8,128)S(1)}, u32[]{:S(2)}, u32[]{:S(2)}) %all-to-all-start.2) | async-done | bytes 2064416 | tf_op jit(solution)/shard_map/all_to_all | solution.py:118
  85.6 6.5 multiply_reduce_fusion
  93.5 6.1 scatter_custom_fusion.3
  107.6 15.4 %copy.132 = f32[192,8,8,256]{3,2,1,0:T(8,128)} copy(f32[192,8,8,256]{3,1,2,0:T(8,128)} %bitcast.619) | data formatting | bytes 25165824
  123.0 66.1 %psum.35 = f32[]{:T(128)} all-reduce(f32[]{:T(128)} %multiply_reduce_fusion.10), channel_id=1, replica_groups=mesh['trk'=16,'mod'=8] {'trk','mod'}, use_global_device_ids=true, to_apply=%region_15.16 | all-reduce | flops 1 | bytes 8 | tf_op jit(solution)/shard_map/psum | solution.py:65
  191.5 817.6 %while.14 = (s32[]{:T(128)}, f32[64,16384]{1,0:T(8,128)}, f32[8,256,64]{2,1,0:T(8,128)}, f32[8,256,12,128]{1,0,3,2:T(8,128)}, f32[8,256,12,12]{1,0,3,2:T(8,128)S(1)}, /*index=5*/s32[]{:T(128)}, s32[]{:T(128)}) while((s32[]{:T(128)}, f32[64,16384]{1,0:T(8,128)}, f32[8,256,64]{2,1,0:T(8,128)}, f32[8,256,12,128]{1,0,3,2:T(8,128)}, ...), condition=%wide.region_11.12_spmd.clone, body=%wide.region_10.11_spmd.clone.sunk | while | flops 3328835584 | bytes 85672776 | solution.py:164
  195.9 6.0 constant_dynamic-slice_fusion.5
  211.4 52.4 %multiply_add_fusion.4 = f32[256,128,128]{2,1,0:T(8,128)S(1)} fusion(f32[256,128]{1,0:T(8,128)S(1)} %add_bitcast_fusion.24, f32[256,128]{1,0:T(8,128)S(1)} %get-tuple-element.551, f32[256,128]{1,0:T(8,128)S(1)} %add_bitcast_fusion.25, f32[256,128]{1,0:T(8,128)S(1)} %get-tuple-element.564, f32[256,128]{1,0:T(8,128)S(1)} %add_bitcast_fusion.26, ...), kind=kLoop, calls=%fused_computation.11.clone.1 | loop fusion | flops 96468992 | bytes 19922944 | tf_op jit(solution)/shard_map/while/body/eval_jaxpr/add | solution.py:153
  263.8 28.4 %convolution_add_fusion.2 = f32[64,16384]{1,0:T(8,128)} fusion(f32[32,8,128,128]{3,2,1,0:T(8,128)S(1)} %bitcast.617, f32[64,16384]{1,0:T(8,128)} %get-tuple-element.703, pred[]{:T(512)S(6)} %compare.26, f32[8,256,64]{2,1,0:T(8,128)} %get-tuple-element.711, s32[]{:T(128)S(6)} %copy.153), kind=kOutput, calls=%fused_computation.8.clone.1 | convolution fusion | flops 3223322624 | bytes 25296900 | tf_op jit(solution)/shard_map/while/body/eval_jaxpr/dot_general | solution.py:157
  296.3 6.0 constant_dynamic-slice_fusion.5
  311.7 52.4 %multiply_add_fusion.4 = f32[256,128,128]{2,1,0:T(8,128)S(1)} fusion(f32[256,128]{1,0:T(8,128)S(1)} %add_bitcast_fusion.24, f32[256,128]{1,0:T(8,128)S(1)} %get-tuple-element.551, f32[256,128]{1,0:T(8,128)S(1)} %add_bitcast_fusion.25, f32[256,128]{1,0:T(8,128)S(1)} %get-tuple-element.564, f32[256,128]{1,0:T(8,128)S(1)} %add_bitcast_fusion.26, ...), kind=kLoop, calls=%fused_computation.11.clone.1 | loop fusion | flops 96468992 | bytes 19922944 | tf_op jit(solution)/shard_map/while/body/eval_jaxpr/add | solution.py:153
  364.2 29.0 %convolution_add_fusion.2 = f32[64,16384]{1,0:T(8,128)} fusion(f32[32,8,128,128]{3,2,1,0:T(8,128)S(1)} %bitcast.617, f32[64,16384]{1,0:T(8,128)} %get-tuple-element.703, pred[]{:T(512)S(6)} %compare.26, f32[8,256,64]{2,1,0:T(8,128)} %get-tuple-element.711, s32[]{:T(128)S(6)} %copy.153), kind=kOutput, calls=%fused_computation.8.clone.1 | convolution fusion | flops 3223322624 | bytes 25296900 | tf_op jit(solution)/shard_map/while/body/eval_jaxpr/dot_general | solution.py:157
  397.3 6.0 constant_dynamic-slice_fusion.5
  412.7 52.4 %multiply_add_fusion.4 = f32[256,128,128]{2,1,0:T(8,128)S(1)} fusion(f32[256,128]{1,0:T(8,128)S(1)} %add_bitcast_fusion.24, f32[256,128]{1,0:T(8,128)S(1)} %get-tuple-element.551, f32[256,128]{1,0:T(8,128)S(1)} %add_bitcast_fusion.25, f32[256,128]{1,0:T(8,128)S(1)} %get-tuple-element.564, f32[256,128]{1,0:T(8,128)S(1)} %add_bitcast_fusion.26, ...), kind=kLoop, calls=%fused_computation.11.clone.1 | loop fusion | flops 96468992 | bytes 19922944 | tf_op jit(solution)/shard_map/while/body/eval_jaxpr/add | solution.py:153
  465.2 29.0 %convolution_add_fusion.2 = f32[64,16384]{1,0:T(8,128)} fusion(f32[32,8,128,128]{3,2,1,0:T(8,128)S(1)} %bitcast.617, f32[64,16384]{1,0:T(8,128)} %get-tuple-element.703, pred[]{:T(512)S(6)} %compare.26, f32[8,256,64]{2,1,0:T(8,128)} %get-tuple-element.711, s32[]{:T(128)S(6)} %copy.153), kind=kOutput, calls=%fused_computation.8.clone.1 | convolution fusion | flops 3223322624 | bytes 25296900 | tf_op jit(solution)/shard_map/while/body/eval_jaxpr/dot_general | solution.py:157
  498.3 6.0 constant_dynamic-slice_fusion.5
  513.7 52.4 %multiply_add_fusion.4 = f32[256,128,128]{2,1,0:T(8,128)S(1)} fusion(f32[256,128]{1,0:T(8,128)S(1)} %add_bitcast_fusion.24, f32[256,128]{1,0:T(8,128)S(1)} %get-tuple-element.551, f32[256,128]{1,0:T(8,128)S(1)} %add_bitcast_fusion.25, f32[256,128]{1,0:T(8,128)S(1)} %get-tuple-element.564, f32[256,128]{1,0:T(8,128)S(1)} %add_bitcast_fusion.26, ...), kind=kLoop, calls=%fused_computation.11.clone.1 | loop fusion | flops 96468992 | bytes 19922944 | tf_op jit(solution)/shard_map/while/body/eval_jaxpr/add | solution.py:153
  566.2 29.0 %convolution_add_fusion.2 = f32[64,16384]{1,0:T(8,128)} fusion(f32[32,8,128,128]{3,2,1,0:T(8,128)S(1)} %bitcast.617, f32[64,16384]{1,0:T(8,128)} %get-tuple-element.703, pred[]{:T(512)S(6)} %compare.26, f32[8,256,64]{2,1,0:T(8,128)} %get-tuple-element.711, s32[]{:T(128)S(6)} %copy.153), kind=kOutput, calls=%fused_computation.8.clone.1 | convolution fusion | flops 3223322624 | bytes 25296900 | tf_op jit(solution)/shard_map/while/body/eval_jaxpr/dot_general | solution.py:157
  599.3 6.0 constant_dynamic-slice_fusion.5
  614.7 52.4 %multiply_add_fusion.4 = f32[256,128,128]{2,1,0:T(8,128)S(1)} fusion(f32[256,128]{1,0:T(8,128)S(1)} %add_bitcast_fusion.24, f32[256,128]{1,0:T(8,128)S(1)} %get-tuple-element.551, f32[256,128]{1,0:T(8,128)S(1)} %add_bitcast_fusion.25, f32[256,128]{1,0:T(8,128)S(1)} %get-tuple-element.564, f32[256,128]{1,0:T(8,128)S(1)} %add_bitcast_fusion.26, ...), kind=kLoop, calls=%fused_computation.11.clone.1 | loop fusion | flops 96468992 | bytes 19922944 | tf_op jit(solution)/shard_map/while/body/eval_jaxpr/add | solution.py:153
  667.2 29.0 %convolution_add_fusion.2 = f32[64,16384]{1,0:T(8,128)} fusion(f32[32,8,128,128]{3,2,1,0:T(8,128)S(1)} %bitcast.617, f32[64,16384]{1,0:T(8,128)} %get-tuple-element.703, pred[]{:T(512)S(6)} %compare.26, f32[8,256,64]{2,1,0:T(8,128)} %get-tuple-element.711, s32[]{:T(128)S(6)} %copy.153), kind=kOutput, calls=%fused_computation.8.clone.1 | convolution fusion | flops 3223322624 | bytes 25296900 | tf_op jit(solution)/shard_map/while/body/eval_jaxpr/dot_general | solution.py:157
  700.3 6.0 constant_dynamic-slice_fusion.5
  715.8 52.4 %multiply_add_fusion.4 = f32[256,128,128]{2,1,0:T(8,128)S(1)} fusion(f32[256,128]{1,0:T(8,128)S(1)} %add_bitcast_fusion.24, f32[256,128]{1,0:T(8,128)S(1)} %get-tuple-element.551, f32[256,128]{1,0:T(8,128)S(1)} %add_bitcast_fusion.25, f32[256,128]{1,0:T(8,128)S(1)} %get-tuple-element.564, f32[256,128]{1,0:T(8,128)S(1)} %add_bitcast_fusion.26, ...), kind=kLoop, calls=%fused_computation.11.clone.1 | loop fusion | flops 96468992 | bytes 19922944 | tf_op jit(solution)/shard_map/while/body/eval_jaxpr/add | solution.py:153
  768.2 29.0 %convolution_add_fusion.2 = f32[64,16384]{1,0:T(8,128)} fusion(f32[32,8,128,128]{3,2,1,0:T(8,128)S(1)} %bitcast.617, f32[64,16384]{1,0:T(8,128)} %get-tuple-element.703, pred[]{:T(512)S(6)} %compare.26, f32[8,256,64]{2,1,0:T(8,128)} %get-tuple-element.711, s32[]{:T(128)S(6)} %copy.153), kind=kOutput, calls=%fused_computation.8.clone.1 | convolution fusion | flops 3223322624 | bytes 25296900 | tf_op jit(solution)/shard_map/while/body/eval_jaxpr/dot_general | solution.py:157
  801.3 6.0 constant_dynamic-slice_fusion.5
  816.8 52.4 %multiply_add_fusion.4 = f32[256,128,128]{2,1,0:T(8,128)S(1)} fusion(f32[256,128]{1,0:T(8,128)S(1)} %add_bitcast_fusion.24, f32[256,128]{1,0:T(8,128)S(1)} %get-tuple-element.551, f32[256,128]{1,0:T(8,128)S(1)} %add_bitcast_fusion.25, f32[256,128]{1,0:T(8,128)S(1)} %get-tuple-element.564, f32[256,128]{1,0:T(8,128)S(1)} %add_bitcast_fusion.26, ...), kind=kLoop, calls=%fused_computation.11.clone.1 | loop fusion | flops 96468992 | bytes 19922944 | tf_op jit(solution)/shard_map/while/body/eval_jaxpr/add | solution.py:153
  869.2 29.0 %convolution_add_fusion.2 = f32[64,16384]{1,0:T(8,128)} fusion(f32[32,8,128,128]{3,2,1,0:T(8,128)S(1)} %bitcast.617, f32[64,16384]{1,0:T(8,128)} %get-tuple-element.703, pred[]{:T(512)S(6)} %compare.26, f32[8,256,64]{2,1,0:T(8,128)} %get-tuple-element.711, s32[]{:T(128)S(6)} %copy.153), kind=kOutput, calls=%fused_computation.8.clone.1 | convolution fusion | flops 3223322624 | bytes 25296900 | tf_op jit(solution)/shard_map/while/body/eval_jaxpr/dot_general | solution.py:157
  902.3 6.0 constant_dynamic-slice_fusion.5
  917.8 52.4 %multiply_add_fusion.4 = f32[256,128,128]{2,1,0:T(8,128)S(1)} fusion(f32[256,128]{1,0:T(8,128)S(1)} %add_bitcast_fusion.24, f32[256,128]{1,0:T(8,128)S(1)} %get-tuple-element.551, f32[256,128]{1,0:T(8,128)S(1)} %add_bitcast_fusion.25, f32[256,128]{1,0:T(8,128)S(1)} %get-tuple-element.564, f32[256,128]{1,0:T(8,128)S(1)} %add_bitcast_fusion.26, ...), kind=kLoop, calls=%fused_computation.11.clone.1 | loop fusion | flops 96468992 | bytes 19922944 | tf_op jit(solution)/shard_map/while/body/eval_jaxpr/add | solution.py:153
  970.2 29.0 %convolution_add_fusion.2 = f32[64,16384]{1,0:T(8,128)} fusion(f32[32,8,128,128]{3,2,1,0:T(8,128)S(1)} %bitcast.617, f32[64,16384]{1,0:T(8,128)} %get-tuple-element.703, pred[]{:T(512)S(6)} %compare.26, f32[8,256,64]{2,1,0:T(8,128)} %get-tuple-element.711, s32[]{:T(128)S(6)} %copy.153), kind=kOutput, calls=%fused_computation.8.clone.1 | convolution fusion | flops 3223322624 | bytes 25296900 | tf_op jit(solution)/shard_map/while/body/eval_jaxpr/dot_general | solution.py:157
  1009.1 4.9 copy.134
  1014.9 2.8 gather_fusion
  1018.0 3.3 multiply_reduce_fusion.2
  1021.7 6.2 scatter_custom_fusion.4
  1030.9 69.1 %psum.36 = f32[]{:T(128)} all-reduce(f32[]{:T(128)} %multiply_reduce_fusion.9), channel_id=1, replica_groups=mesh['trk'=16,'mod'=8] {'trk','mod'}, use_global_device_ids=true, to_apply=%region_19.20 | all-reduce | flops 1 | bytes 8 | tf_op jit(solution)/shard_map/psum | solution.py:65
  1101.4 62.5 %psum.37 = f32[]{:T(128)} all-reduce(f32[]{:T(128)} %get-tuple-element.140), channel_id=1, replica_groups=mesh['trk'=16,'mod'=8] {'trk','mod'}, use_global_device_ids=true, to_apply=%region_21.22 | all-reduce | flops 1 | bytes 8 | tf_op jit(solution)/shard_map/psum | solution.py:65
  1165.2 2.4 collective-permute-done.3
  1167.8 2.8 gather_fusion.1
  1170.8 3.3 multiply_reduce_fusion.1
  1174.5 6.2 scatter_custom_fusion.5
  1183.8 69.2 %psum.38 = f32[]{:T(128)} all-reduce(f32[]{:T(128)} %multiply_reduce_fusion.7), channel_id=1, replica_groups=mesh['trk'=16,'mod'=8] {'trk','mod'}, use_global_device_ids=true, to_apply=%region_25.26 | all-reduce | flops 1 | bytes 8 | tf_op jit(solution)/shard_map/psum | solution.py:65
  1257.3 62.6 %psum.39 = f32[]{:T(128)} all-reduce(f32[]{:T(128)} %multiply_reduce_fusion.6), channel_id=1, replica_groups=mesh['trk'=16,'mod'=8] {'trk','mod'}, use_global_device_ids=true, to_apply=%region_27.28 | all-reduce | flops 1 | bytes 8 | tf_op jit(solution)/shard_map/psum | solution.py:65
  (732 shorter events, 151.8 us)
Async XLA Ops:
  0.6 50.4 %copy-start.30 = (s32[64]{0:T(128)S(1)}, s32[64]{0:T(128)}, u32[]{:S(2)}) copy-start(s32[64]{0:T(128)} %param.24) | copy-start | bytes 772
  5.2 21.1 %all-to-all-start = ((s32[128,16,1]{1,2,0:T(1,128)}), s32[128,16,1]{1,2,0:T(1,128)S(1)}, u32[]{:S(2)}, u32[]{:S(2)}) async-start(s32[128,16,1]{1,2,0:T(1,128)} %bitcast.4), calls=%async_computation | async-start | bytes 131072 | tf_op jit(solution)/shard_map/all_to_all | solution.py:120
  26.2 19.7 %all-to-all-start.1 = ((s32[128,1,192]{2,1,0:T(1,128)}), s32[128,1,192]{2,1,0:T(1,128)S(1)}, u32[]{:S(2)}, u32[]{:S(2)}) async-start(s32[128,1,192]{2,1,0:T(1,128)} %reshape.2217), calls=%async_computation.1 | async-start | bytes 262144 | tf_op jit(solution)/shard_map/all_to_all | solution.py:119
  45.9 35.5 %all-to-all-start.2 = ((f32[128,16,252]{2,1,0:T(8,128)}), f32[128,16,252]{2,1,0:T(8,128)S(1)}, u32[]{:S(2)}, u32[]{:S(2)}) async-start(f32[128,16,252]{2,1,0:T(8,128)} %bitcast.633), calls=%async_computation.2 | async-start | bytes 4194304 | tf_op jit(solution)/shard_map/all_to_all | solution.py:118
  51.4 42.1 %copy-start.29 = (s32[1024,1]{0,1:T(1,128)}, s32[1024,1]{0,1:T(1,128)S(1)}, u32[]{:S(2)}) copy-start(s32[1024,1]{0,1:T(1,128)S(1)} %compare_select_fusion.1) | copy-start | bytes 12292
  99.7 7.1 collective-permute-start
  107.0 1214.3 %copy-start.2 = (f32[512,8]{0,1:T(8,128)}, f32[512,8]{0,1:T(8,128)S(1)}, u32[]{:S(2)}) copy-start(f32[512,8]{0,1:T(8,128)S(1)} %scatter-add.37) | copy-start | bytes 49156
  190.4 823.7 %collective-permute-start.1 = (f32[16,8]{0,1:T(8,128)}, f32[16,8]{0,1:T(8,128)}, u32[]{:S(2)}, u32[]{:S(2)}) collective-permute-start(f32[16,8]{0,1:T(8,128)} %slice.1150), channel_id=1, source_target_pairs={{0,127},{1,0},{2,1},{3,2},{4,3},{5,4},{6,5},{7,6},{8,7},{9,8},{10,... | collective-permute-start | bytes 1544 | tf_op jit(solution)/shard_map/ppermute | solution.py:19
  203.0 6.7 copy-start.4
  203.0 6.7 copy-start.5
  203.0 6.7 copy-start.18
  203.0 6.7 copy-start.19
  263.8 28.4 %copy-start.1 = (f32[8,256,12,12]{1,0,3,2:T(8,128)S(1)}, f32[8,256,12,12]{1,0,3,2:T(8,128)}, u32[]{:S(2)}) copy-start(f32[8,256,12,12]{1,0,3,2:T(8,128)} %copy-done) | copy-start | bytes 3538948 | tf_op jit(solution)/shard_map/while
  303.3 6.7 copy-start.4
  303.3 6.7 copy-start.5
  303.3 6.7 copy-start.18
  303.4 6.7 copy-start.19
  303.4 6.7 copy-start.20
  303.4 6.7 copy-start.21
  303.4 6.7 copy-start.22
  303.4 6.7 copy-start.23
  303.4 6.7 copy-start.24
  303.4 6.7 copy-start.25
  303.4 6.7 copy-start.26
  303.4 6.7 copy-start.27
  364.1 29.0 %copy-start.1 = (f32[8,256,12,12]{1,0,3,2:T(8,128)S(1)}, f32[8,256,12,12]{1,0,3,2:T(8,128)}, u32[]{:S(2)}) copy-start(f32[8,256,12,12]{1,0,3,2:T(8,128)} %copy-done) | copy-start | bytes 3538948 | tf_op jit(solution)/shard_map/while
  465.1 29.0 %copy-start.1 = (f32[8,256,12,12]{1,0,3,2:T(8,128)S(1)}, f32[8,256,12,12]{1,0,3,2:T(8,128)}, u32[]{:S(2)}) copy-start(f32[8,256,12,12]{1,0,3,2:T(8,128)} %copy-done) | copy-start | bytes 3538948 | tf_op jit(solution)/shard_map/while
  566.1 29.0 %copy-start.1 = (f32[8,256,12,12]{1,0,3,2:T(8,128)S(1)}, f32[8,256,12,12]{1,0,3,2:T(8,128)}, u32[]{:S(2)}) copy-start(f32[8,256,12,12]{1,0,3,2:T(8,128)} %copy-done) | copy-start | bytes 3538948 | tf_op jit(solution)/shard_map/while
  667.2 29.0 %copy-start.1 = (f32[8,256,12,12]{1,0,3,2:T(8,128)S(1)}, f32[8,256,12,12]{1,0,3,2:T(8,128)}, u32[]{:S(2)}) copy-start(f32[8,256,12,12]{1,0,3,2:T(8,128)} %copy-done) | copy-start | bytes 3538948 | tf_op jit(solution)/shard_map/while
  707.3 6.7 copy-start.4
  707.3 6.7 copy-start.5
  707.4 6.7 copy-start.18
  707.4 6.7 copy-start.19
  707.4 6.7 copy-start.20
  707.4 6.7 copy-start.21
  707.4 6.7 copy-start.22
  707.4 6.7 copy-start.23
  707.4 6.7 copy-start.24
  707.4 6.7 copy-start.25
  707.4 6.7 copy-start.26
  707.4 6.7 copy-start.27
  768.2 29.0 %copy-start.1 = (f32[8,256,12,12]{1,0,3,2:T(8,128)S(1)}, f32[8,256,12,12]{1,0,3,2:T(8,128)}, u32[]{:S(2)}) copy-start(f32[8,256,12,12]{1,0,3,2:T(8,128)} %copy-done) | copy-start | bytes 3538948 | tf_op jit(solution)/shard_map/while
  869.2 29.0 %copy-start.1 = (f32[8,256,12,12]{1,0,3,2:T(8,128)S(1)}, f32[8,256,12,12]{1,0,3,2:T(8,128)}, u32[]{:S(2)}) copy-start(f32[8,256,12,12]{1,0,3,2:T(8,128)} %copy-done) | copy-start | bytes 3538948 | tf_op jit(solution)/shard_map/while
  970.2 29.0 %copy-start.1 = (f32[8,256,12,12]{1,0,3,2:T(8,128)S(1)}, f32[8,256,12,12]{1,0,3,2:T(8,128)}, u32[]{:S(2)}) copy-start(f32[8,256,12,12]{1,0,3,2:T(8,128)} %copy-done) | copy-start | bytes 3538948 | tf_op jit(solution)/shard_map/while
  1009.1 21.2 %copy-start.3 = (f32[512,8]{0,1:T(8,128)S(1)}, f32[512,8]{0,1:T(8,128)}, u32[]{:S(2)}) copy-start(f32[512,8]{0,1:T(8,128)} %param.25) | copy-start | bytes 49156
  1027.9 2.2 collective-permute-start.2
  1164.5 3.1 collective-permute-start.3
  1180.7 2.3 collective-permute-start.4
  (173 other events, 1090.0 us)
where the time goes:
time: 1330 us; the launch traced here: 1320 us
  other arithmetic  533 us (40%)
  blocking collectives  329 us (25%)
  matrix products  233 us (18%)
  local copies, waits for them, and re-layouts  142 us (11%)
  waiting for transfers between devices  31.7 us (2%)
  starting transfers between devices  30 us (2%)
  loops' own time  14.6 us (1%)
    add x8, other arithmetic, accumulate(): outer = outer + part_laid[:, row_num][:, :, None] * mixed_row[:, None, :]  419 us
    psum x5, blocking collectives, global_sum(): return lax.psum(local_term, ('trk', 'mod'))  329 us
    dot_general x8, matrix products, accumulate(): jnp.dot(part_road.T, flat_outer, precision=HIGHEST, preferred_element_typ...  232 us
    mul x96, other arithmetic, accumulate(): outer = outer + part_laid[:, row_num][:, :, None] * mixed_row[:, None, :]  62.8 us
    dynamic_slice x32, local copies, waits for them, and re-layouts, on_device(): lax.scan(accumulate, start_total, (laid.reshape(block_count, rows_each, N...  56.5 us
    slice x64, local copies, waits for them, and re-layouts, accumulate(): part_schur[:, row_num, col_num][:, None] * part_laid[:, col_num]  31.3 us
  transfers between devices with their start and end apart: 8, of which 6 were waited for; matrix products, arithmetic and copies ran while one was open for 63% of the time, Pallas kernels for 0%

commit v1 on v0

v1 whole, which is shorter than its diff:
```python
import functools

import jax
import jax.numpy as jnp
from jax import lax
from jax.experimental import pallas as pl
from jax.experimental.pallas import tpu as pltpu
from jax.sharding import PartitionSpec as P

F32 = jnp.float32
BF16 = jnp.bfloat16
NPAR = 8
NLOC = 5
NHIT = 12
ROAD = 16
CAP = 16
LANE = 128
NMOD = 65536
ROADS = 64
TRACKS = 512
DEV = 128
GROUP = 16
EPS = 1e-6
MESH = pl.DeviceIdType.MESH
CONTRACT_LANES = (((1,), (1,)), ((), ()))


def dot_t(a, b):
    return lax.dot_general(a, b, CONTRACT_LANES, preferred_element_type=F32)


def split(x):
    hi = x.astype(BF16)
    return hi, (x - hi.astype(F32)).astype(BF16)


def fit_and_place(ld, gd, me, hw, hm, hc, tr, send, lay):
    position = lax.broadcasted_iota(jnp.int32, (NHIT, TRACKS), 0)
    live = position < hc[...]
    root = jnp.where(live, jnp.sqrt(hw[...]), 0.0)
    scaled = [ld[a] * root for a in range(NLOC)]
    factor = {}
    for i in range(NLOC):
        for j in range(i + 1):
            running = jnp.sum(scaled[i] * scaled[j], axis=0, keepdims=True)
            if i == j:
                running = running + 1.0
            for k in range(j):
                running = running - factor[i, k] * factor[j, k]
            factor[i, j] = jnp.sqrt(running) if i == j else running / factor[j, j]
    proj = []
    for i in range(NLOC):
        running = scaled[i]
        for j in range(i):
            running = running - factor[i, j] * proj[j]
        proj.append(running / factor[i, i])
    resid = me[...] * root
    solved = resid
    for a in range(NLOC):
        solved = solved - proj[a] * jnp.sum(proj[a] * resid, axis=0, keepdims=True)
    road = tr[...]
    rel = lax.rem(hm[...] - NPAR * road + NMOD, NMOD).astype(F32)
    local_road = jnp.broadcast_to((road & (ROADS - 1)).astype(F32), (NHIT, TRACKS))
    words = [gd[p] * root for p in range(NPAR)] + proj + [solved, rel, local_road]
    for w, value in enumerate(words):
        for c in range(TRACKS // LANE):
            part = value[:, c * LANE : (c + 1) * LANE]
            lay[c, pl.ds(w, 8, stride=16), :] = part[:8]
            lay[c, pl.ds(LANE + w, 4, stride=16), :] = part[8:]
    whole = jnp.concatenate([lay[c] for c in range(TRACKS // LANE)], axis=1)
    first_hi, first_lo = split(whole[:LANE])
    tail = whole[LANE:]
    none = jnp.zeros_like(tail)
    left_hi, left_lo = split(jnp.concatenate([tail, none], axis=0))
    right_hi, right_lo = split(jnp.concatenate([none, tail], axis=0))

    owner = road >> 6
    mine = lax.broadcasted_iota(jnp.int32, (DEV, TRACKS), 0) == owner
    member = jnp.where(mine, 1.0, 0.0)
    earlier = lax.broadcasted_iota(jnp.int32, (TRACKS, TRACKS), 0) <= lax.broadcasted_iota(
        jnp.int32, (TRACKS, TRACKS), 1
    )
    running = jnp.dot(
        member.astype(BF16), jnp.where(earlier, 1.0, 0.0).astype(BF16), preferred_element_type=F32
    )
    rank = jnp.sum(member * running, axis=0, keepdims=True) - 1.0
    slot = owner * CAP + rank.astype(jnp.int32)

    def place(step, carry):
        row = lax.broadcasted_iota(jnp.int32, (GROUP * CAP, TRACKS), 0) + step * (GROUP * CAP)
        chosen = jnp.where(row == slot, 1.0, 0.0)
        pick = chosen.astype(BF16)
        first = dot_t(pick, first_hi) + dot_t(pick, first_lo)
        halves = chosen.reshape(GROUP, 2, 8, TRACKS)
        low = halves[:, 0].reshape(LANE, TRACKS).astype(BF16)
        high = halves[:, 1].reshape(LANE, TRACKS).astype(BF16)
        last = dot_t(low, left_hi) + dot_t(low, left_lo) + dot_t(high, right_hi) + dot_t(high, right_lo)
        at = pl.ds(pl.multiple_of(step * GROUP, GROUP), GROUP)
        send[at, 0:16, :] = first.reshape(GROUP, CAP, LANE)
        send[at, 16:24, :] = last.reshape(GROUP, 8, LANE)
        return carry

    lax.fori_loop(0, DEV // GROUP, place, 0)


def kernel_send(ld, gd, me, hw, hm, hc, tr, send, lay):
    fit_and_place(ld, gd, me, hw, hm, hc, tr, send, lay)


def assemble(x, off, blocks, road_rhs, g_ref, x_ref, hot_ref, mix_ref, z_ref):
    t0 = x[:, 0:8, :].reshape(LANE, LANE).T
    t1 = x[:, 8:16, :].reshape(LANE, LANE).T
    t2 = x[:, 16:24, :].reshape(LANE, LANE).T
    body = jnp.concatenate([t0, t1], axis=1)
    tail = jnp.concatenate([t2[:64], t2[64:]], axis=1)
    hits = []
    for i in range(NHIT):
        source, row = (body, 16 * i) if i < 8 else (tail, 16 * (i - 8))
        hits.append((source[row : row + 8], source[row + 8 : row + 16]))
    wide = 2 * LANE
    road = hits[0][1][7:8]
    each = lax.broadcasted_iota(jnp.int32, (ROADS, wide), 0).astype(F32)
    hot = jnp.where(each == road, 1.0, 0.0)
    start = jnp.sum(hot * off, axis=0, keepdims=True)
    rows = (lax.broadcasted_iota(jnp.int32, (ROADS * NPAR, wide), 0) >> 3).astype(F32)
    hot_ref[...] = jnp.where(rows == road, 1.0, 0.0).astype(BF16)
    slots = [jnp.broadcast_to(hits[i][1][6:7] - start, (8, wide)) for i in range(NHIT)]
    sums = []
    for s in range(ROAD):
        g = jnp.zeros((8, wide), F32)
        a = jnp.zeros((8, wide), F32)
        for i in range(NHIT):
            same = slots[i] == float(s)
            g = jnp.where(same, hits[i][0], g)
            a = jnp.where(same, hits[i][1], a)
        g_ref[8 * s : 8 * s + 8, :] = g
        x_ref[0, 8 * s : 8 * s + 8, :] = a[:, :LANE]
        x_ref[1, 8 * s : 8 * s + 8, :] = a[:, LANE:]
        sums.append(g * a[5:6])
    v_hi, v_lo = split(jnp.concatenate(sums, axis=0))
    hot16 = hot.astype(BF16)
    road_rhs[...] += dot_t(hot16, v_hi) + dot_t(hot16, v_lo)
    lines = [
        jnp.concatenate(
            [x_ref[c, pl.ds(a, ROAD, stride=8), :] for c in range(2)], axis=1
        )
        for a in range(NLOC)
    ]

    def slot_step(s, carry):
        at = pl.ds(pl.multiple_of(s * 8, 8), 8)
        g_s = g_ref[at, :]
        a_s = jnp.concatenate([x_ref[0, at, :], x_ref[1, at, :]], axis=1)
        mix = jnp.where(lax.broadcasted_iota(jnp.int32, (ROAD, wide), 0) == s, 1.0, 0.0)
        for a in range(NLOC):
            mix = mix - a_s[a : a + 1] * lines[a]
        mix_ref[...] = mix
        for u in range(ROAD):
            z = g_ref[8 * u : 8 * u + 8, :] * mix_ref[u : u + 1, :]
            z_ref[8 * u : 8 * u + 8, :] = z
        z_hi, z_lo = split(z_ref[...])
        pair = jnp.concatenate([g_s, g_s], axis=0)
        g_hi, g_lo = split(pair)
        hot = hot_ref[...].reshape(ROADS // 2, 16, wide)
        left_hi = (hot * g_hi[None]).reshape(ROADS * NPAR, wide)
        left_lo = (hot * g_lo[None]).reshape(ROADS * NPAR, wide)
        out = dot_t(left_hi, z_hi) + dot_t(left_hi, z_lo) + dot_t(left_lo, z_hi)
        blocks[:, at, :] += out.reshape(ROADS, NPAR, LANE)
        return carry

    lax.fori_loop(0, ROAD, slot_step, 0)


def kernel_assemble(x, off, blocks, road_rhs, g_ref, x_ref, hot_ref, mix_ref, z_ref):
    @pl.when(pl.program_id(0) == 0)
    def _():
        blocks[...] = jnp.zeros_like(blocks)
        road_rhs[...] = jnp.zeros_like(road_rhs)

    assemble(x[...], off[...], blocks, road_rhs, g_ref, x_ref, hot_ref, mix_ref, z_ref)


HALF = 64


def low_lanes(x):
    return jnp.where(lax.broadcasted_iota(jnp.int32, x.shape, 1) < HALF, x, 0.0)


def spread(pieces, off, field):
    wide = jnp.concatenate([pieces, jnp.zeros_like(pieces)], axis=1)
    moved = jnp.where(off == 0.0, wide, 0.0)
    for d in range(1, NPAR):
        moved = jnp.where(off == float(d), pltpu.roll(wide, 8 * d, 1), moved)
    head, rest = moved[:, :LANE], moved[:, LANE:]
    field[...] = jnp.zeros_like(field)
    field[0:64, :] = low_lanes(head)
    field[1:65, :] += low_lanes(pltpu.roll(head, HALF, 1))
    field[2:66, :] += low_lanes(rest)


def gather(field, off):
    head = field[0:64, :] + pltpu.roll(field[1:65, :], HALF, 1)
    wide = jnp.concatenate([head, field[2:66, :]], axis=1)
    piece = jnp.where(off == 0.0, wide, 0.0)
    for d in range(1, NPAR):
        piece = jnp.where(off == float(d), pltpu.roll(wide, 2 * LANE - 8 * d, 1), piece)
    return piece[:, :LANE]


def total(x):
    return jnp.sum(jnp.sum(x, axis=0, keepdims=True), axis=1, keepdims=True)


def krylov(blocks, road_rhs, off, prior, rhs_out, cor_out, field, vec, image, mapped, up, down,
           from_prev, from_next, line, lines, sems, gsem):
    trk, mod = lax.axis_index("trk"), lax.axis_index("mod")
    me = trk * 8 + mod
    nxt = lax.rem(me + 1, DEV)
    prv = lax.rem(me + DEV - 1, DEV)
    off = off[...]

    def place(d):
        return (d // 8, lax.rem(d, 8))

    def exchange(e, target):
        up[e] = field[64:72, :]
        down[e] = field[0:8, :]
        to_next = pltpu.make_async_remote_copy(
            up.at[e], from_prev.at[e], sems.at[e, 0], sems.at[e, 1], device_id=place(nxt), device_id_type=MESH
        )
        to_prev = pltpu.make_async_remote_copy(
            down.at[e], from_next.at[e], sems.at[e, 2], sems.at[e, 3], device_id=place(prv), device_id_type=MESH
        )
        to_next.start()
        to_prev.start()
        target[8:64, :] = field[8:64, :]
        to_next.wait()
        to_prev.wait()
        keep = lax.broadcasted_iota(jnp.int32, (8, LANE), 0) < 2
        target[0:8, :] = field[0:8, :] + jnp.where(keep, from_prev[e], 0.0)
        target[64:72, :] = jnp.where(keep, field[64:72, :] + from_next[e], 0.0)

    def apply(source, e, target):
        piece = gather(source, off)
        flipped = piece.T
        for r in range(ROADS):
            row = jnp.sum(blocks[r] * flipped[:, r : r + 1], axis=0, keepdims=True)
            mapped[r : r + 1, :] = row
        spread(mapped[...], off, field)
        field[0:64, :] += prior[...] * source[0:64, :]
        exchange(e, target)

    spread(road_rhs[...], off, field)
    exchange(0, vec.at[0])
    rhs_out[...] = vec[0, 0:64, :]
    apply(vec.at[0], 1, vec.at[1])
    apply(vec.at[1], 2, vec.at[2])
    b, w, u = vec[0, 0:64, :], vec[1, 0:64, :], vec[2, 0:64, :]

    def unit(norm):
        return jnp.where(norm > 0.0, 1.0 / jnp.where(norm > 0.0, norm, 1.0), 0.0)

    r11 = jnp.sqrt(total(b * b))
    q1 = b * unit(r11)
    r12 = total(q1 * w)
    r13 = total(q1 * u)
    w1 = w - r12 * q1
    u1 = u - r13 * q1
    r22 = jnp.sqrt(total(w1 * w1))
    q2 = w1 * unit(r22)
    r23 = total(q2 * u1)
    u2 = u1 - r23 * q2
    r33 = jnp.sqrt(total(u2 * u2))
    lane = lax.broadcasted_iota(jnp.int32, (1, LANE), 1)
    row = jnp.zeros((1, LANE), F32)
    for n, value in enumerate((r11, r12, r13, r22, r23, r33)):
        row = jnp.where(lane == n, value, row)
    line[...] = row
    lines[me] = row

    def send_line(k, carry):
        other = lax.rem(me + k, DEV)
        pltpu.make_async_remote_copy(
            line, lines.at[me], gsem.at[0], gsem.at[1], device_id=place(other), device_id_type=MESH
        ).start()
        return carry

    lax.fori_loop(1, DEV, send_line, 0)
    whole = pltpu.make_async_remote_copy(
        lines.at[pl.ds(0, DEV - 1)], lines.at[pl.ds(0, DEV - 1)], gsem.at[0], gsem.at[1],
        device_id=place(nxt), device_id_type=MESH,
    )
    whole.wait_recv()
    every = lines[...]

    def col(n):
        return every[:, :, n : n + 1]

    def add(x):
        return jnp.sum(x, axis=0)

    b0, w0, u0, w1, u1, u2 = (col(n) for n in range(6))
    beta_one = jnp.sqrt(add(b0 * b0) + EPS)
    inv_one = 1.0 / beta_one
    b0 = b0 * inv_one
    w0, w1 = w0 * inv_one, w1 * inv_one
    u0, u1, u2 = u0 * inv_one, u1 * inv_one, u2 * inv_one
    alpha_one = add(b0 * w0)
    x0, x1 = w0 - alpha_one * b0, w1
    beta_two = jnp.sqrt(add(x0 * x0 + x1 * x1) + EPS)
    inv_two = 1.0 / beta_two
    x0, x1 = x0 * inv_two, x1 * inv_two
    y0 = (u0 - alpha_one * w0) * inv_two - beta_two * b0
    y1 = (u1 - alpha_one * w1) * inv_two
    y2 = u2 * inv_two
    alpha_two = add(x0 * y0 + x1 * y1)
    y0, y1 = y0 - alpha_two * x0, y1 - alpha_two * x1
    beta_three = jnp.sqrt(add(y0 * y0 + y1 * y1 + y2 * y2) + EPS)
    first = alpha_one * alpha_one + beta_two * beta_two
    cross = beta_two * (alpha_one + alpha_two)
    second = beta_two * beta_two + alpha_two * alpha_two + beta_three * beta_three
    determinant = first * second - cross * cross
    coef_one = beta_one * (second * alpha_one - cross * beta_two) / determinant
    coef_two = beta_one * (first * beta_two - cross * alpha_one) / determinant
    v1 = b * inv_one
    v2 = (w * inv_one - alpha_one * v1) * inv_two
    cor_out[...] = coef_one * v1 + coef_two * v2
    whole.wait_send()


def kernel_krylov(*refs):
    trk, mod = lax.axis_index("trk"), lax.axis_index("mod")
    me = trk * 8 + mod
    barrier = pltpu.get_barrier_semaphore()

    def greet(k, carry):
        other = lax.rem(me + k, DEV)
        pl.semaphore_signal(
            barrier, inc=1, device_id=(other // 8, lax.rem(other, 8)), device_id_type=MESH
        )
        return carry

    lax.fori_loop(1, DEV, greet, 0)
    pl.semaphore_wait(barrier, DEV - 1)
    krylov(*refs)


VM = pl.BlockSpec(memory_space=pltpu.VMEM)


def on_device(ld, gd, me, hw, hm, hc, tr, rs, pw):
    send = pl.pallas_call(
        kernel_send,
        out_shape=jax.ShapeDtypeStruct((DEV, 24, LANE), F32),
        in_specs=[VM] * 7,
        out_specs=VM,
        scratch_shapes=[pltpu.VMEM((4, 192, LANE), F32)],
        name="fit_place",
    )(ld, gd, me, hw, hm, hc.reshape(1, TRACKS), tr.reshape(1, TRACKS))
    recv = lax.all_to_all(send, ("trk", "mod"), split_axis=0, concat_axis=0, tiled=True)
    off = (rs % NPAR).astype(F32).reshape(ROADS, 1)
    blocks, road_rhs = pl.pallas_call(
        kernel_assemble,
        grid=(DEV // GROUP,),
        out_shape=(
            jax.ShapeDtypeStruct((ROADS, LANE, LANE), F32),
            jax.ShapeDtypeStruct((ROADS, LANE), F32),
        ),
        in_specs=[
            pl.BlockSpec((GROUP, 24, LANE), lambda c: (c, 0, 0)),
            pl.BlockSpec((ROADS, 1), lambda c: (0, 0)),
        ],
        out_specs=(
            pl.BlockSpec((ROADS, LANE, LANE), lambda c: (0, 0, 0)),
            pl.BlockSpec((ROADS, LANE), lambda c: (0, 0)),
        ),
        scratch_shapes=[
            pltpu.VMEM((LANE, 2 * LANE), F32),
            pltpu.VMEM((2, LANE, LANE), F32),
            pltpu.VMEM((ROADS * NPAR, 2 * LANE), BF16),
            pltpu.VMEM((ROAD, 2 * LANE), F32),
            pltpu.VMEM((LANE, 2 * LANE), F32),
        ],
        name="assemble",
    )(recv, off)
    prior = jnp.pad(pw.reshape(HALF, HALF), ((0, 0), (0, HALF)))
    rhs, cor = pl.pallas_call(
        kernel_krylov,
        out_shape=(jax.ShapeDtypeStruct((HALF, LANE), F32), jax.ShapeDtypeStruct((HALF, LANE), F32)),
        in_specs=[VM] * 4,
        out_specs=(VM, VM),
        scratch_shapes=[
            pltpu.VMEM((72, LANE), F32),
            pltpu.VMEM((3, 72, LANE), F32),
            pltpu.VMEM((72, LANE), F32),
            pltpu.VMEM((ROADS, LANE), F32),
            pltpu.VMEM((3, 8, LANE), F32),
            pltpu.VMEM((3, 8, LANE), F32),
            pltpu.VMEM((3, 8, LANE), F32),
            pltpu.VMEM((3, 8, LANE), F32),
            pltpu.VMEM((1, LANE), F32),
            pltpu.VMEM((DEV, 1, LANE), F32),
            pltpu.SemaphoreType.DMA((3, 4)),
            pltpu.SemaphoreType.DMA((2,)),
        ],
        compiler_params=pltpu.CompilerParams(collective_id=0, has_side_effects=True),
        name="krylov",
    )(blocks, road_rhs, off, prior)
    return (
        blocks,
        rhs[:, :HALF].reshape(TRACKS, NPAR),
        cor[:, :HALF].reshape(TRACKS, NPAR),
    )


def solution(mesh):
    both = ("trk", "mod")
    in_specs = (
        P(None, None, both),
        P(None, None, both),
        P(None, both),
        P(None, both),
        P(None, both),
        P(both),
        P(both),
        P(both),
        P(both, None),
    )
    out_specs = (P(both, None, None), P(both, None), P(both, None))
    return jax.shard_map(on_device, mesh=mesh, in_specs=in_specs, out_specs=out_specs, check_vma=False)
```

time: 1330 us -> 141 us (0.11)
  other arithmetic: 533 us -> 0.01 us
  blocking collectives: 329 us -> 0 us
  matrix products: 233 us -> 0 us
  local copies, waits for them, and re-layouts: 142 us -> 7.66 us
  Pallas kernels: 0 us -> 97.3 us
  starting transfers between devices: 30 us -> 11.5 us
  loops' own time: 14.6 us -> 0 us
    add x14 -> x0, other arithmetic: 420 us -> none  [the longest x8 419 us: accumulate(): outer = outer + part_laid[:, row_num][:, :, None] * mixed_row[:, None, :]]
    psum x5 -> x0, blocking collectives: 329 us -> none  [global_sum(): return lax.psum(local_term, ('trk', 'mod'))]
    dot_general x9 -> x0, matrix products: 233 us -> none  [the longest x8 232 us: accumulate(): jnp.dot(part_road.T, flat_outer, precision=HIGHEST, preferred_element_typ...]
    pallas_call x0 -> x3, Pallas kernels: none -> 97.3 us  [the longest x1 57.6 us: on_device(): pl.pallas_call(kernel_assemble, grid=(DEV // GROUP,), out_shape=(jax.Shap...]
    mul x98 -> x0, other arithmetic: 64.5 us -> none  [the longest x96 62.8 us: accumulate(): outer = outer + part_laid[:, row_num][:, :, None] * mixed_row[:, None, :]]
    dynamic_slice x32 -> x0, local copies, waits for them, and re-layouts: 56.5 us -> none  [on_device(): lax.scan(accumulate, start_total, (laid.reshape(block_count, rows_each, N...]
    slice x78 -> x0, local copies, waits for them, and re-layouts: 39.9 us -> none  [the longest x64 31.3 us: accumulate(): part_schur[:, row_num, col_num][:, None] * part_laid[:, col_num]]
    reduce_sum x13 -> x0, other arithmetic: 20.1 us -> none  [the longest x2 6.68 us: apply_normal(): mapped = jnp.sum(normal_blocks * pieces[:, None, :], axis=2)]
  transfers between devices with their start and end apart: 8 -> 1, of which waited for: 6 -> 1; matrix products, arithmetic and copies ran while one was open for 63% -> 1% of each run, Pallas kernels for 0% -> 0%
where the time goes in v1:
time: 141 us; the launch traced here: 140 us
  Pallas kernels  97.3 us (69%)
  waiting for transfers between devices  23.2 us (16%)
  starting transfers between devices  11.5 us (8%)
  local copies, waits for them, and re-layouts  7.66 us (5%)
    pallas_call x1, Pallas kernels, on_device(): pl.pallas_call(kernel_assemble, grid=(DEV // GROUP,), out_shape=(jax.Shap...  57.6 us
    pallas_call x1, Pallas kernels, on_device(): pl.pallas_call(kernel_krylov, out_shape=(jax.ShapeDtypeStruct((HALF, LANE...  33.4 us
    all_to_all x1, waiting for transfers between devices, on_device(): lax.all_to_all(send, ('trk', 'mod'), split_axis=0, concat_axis=0, tiled=T...  23.2 us
    all_to_all x1, starting transfers between devices, on_device(): lax.all_to_all(send, ('trk', 'mod'), split_axis=0, concat_axis=0, tiled=T...  11.5 us
    pallas_call x1, Pallas kernels, on_device(): pl.pallas_call(kernel_send, out_shape=jax.ShapeDtypeStruct((DEV, 24, LANE...  6.34 us
    unnamed x10, local copies, waits for them, and re-layouts  4.45 us
  transfers between devices with their start and end apart: 1, of which 1 were waited for; matrix products, arithmetic and copies ran while one was open for 1% of the time, Pallas kernels for 0%

profile of v1, /device:TPU:1, one launch (start us, length us, event | category | flops | bytes accessed | tf_op | source)
XLA Modules:
  0.0 140.4 jit_solution(17429056055437756674)
XLA Ops:
  0.6 1.7 %copy.18.gd = f32[8,12,512]{2,1,0:T(8,128)} copy(f32[8,12,512]{2,0,1:T(8,128)} %param.10) | data formatting | bytes 393216 | tf_op args[1]
  2.4 6.3 %fit_place.1 = f32[128,24,128]{2,1,0:T(8,128)} custom-call(f32[5,12,512]{2,1,0:T(8,128)} %ld.1, f32[8,12,512]{2,1,0:T(8,128)} %copy.18.gd, f32[12,512]{1,0:T(8,128)} %me.1, f32[12,512]{1,0:T(8,128)} %hw.1, s32[12,512]{1,0:T(8,128)} %hm.1, s32[1,512]{1,0:T(1,128)} %bitcast.8, s32[1,512]{1,0:T(1,128)} %bitcast.9), custom_call_target="tpu_custom_call" | custom-call | tf_op jit(solution)/shard_map/fit_place/pallas_call | solution.py:353
  8.7 0.0 copy-start.2
  8.7 0.0 copy-start.1
  8.7 11.5 %all-to-all-start = ((f32[128,24,128]{2,1,0:T(8,128)}), f32[128,24,128]{2,1,0:T(8,128)S(1)}, u32[]{:S(2)}, u32[]{:S(2)}) async-start(f32[128,24,128]{2,1,0:T(8,128)} %fit_place.1), calls=%async_computation | async-start | bytes 3145728 | tf_op jit(solution)/shard_map/all_to_all | solution.py:361
  20.2 0.0 copy-done.2
  20.2 0.7 copy.19.off.refs_2_
  20.9 0.0 copy-done.1
  21.0 0.1 copy.20
  21.1 0.1 reshape.27
  21.2 0.6 pad.4.refs_3_
  21.8 23.2 %all-to-all-done.x = f32[128,24,128]{2,1,0:T(8,128)S(1)} async-done(((f32[128,24,128]{2,1,0:T(8,128)}), f32[128,24,128]{2,1,0:T(8,128)S(1)}, u32[]{:S(2)}, u32[]{:S(2)}) %all-to-all-start) | async-done | bytes 1572896 | tf_op jit(solution)/shard_map/all_to_all | solution.py:361
  45.1 0.0 copy-start
  45.1 1.2 copy-done
  46.2 57.6 %assemble.1 = (f32[64,128,128]{2,1,0:T(8,128)}, f32[64,128]{1,0:T(8,128)}) custom-call(f32[128,24,128]{2,1,0:T(8,128)} %copy-done, f32[64,1]{1,0:T(8,128)} %copy.19.off.refs_2_), custom_call_target="tpu_custom_call" | custom-call | tf_op jit(solution)/shard_map/assemble/pallas_call | solution.py:363
  103.8 33.4 %krylov.1 = (f32[64,128]{1,0:T(8,128)}, f32[64,128]{1,0:T(8,128)}) custom-call(f32[64,128,128]{2,1,0:T(8,128)} %get-tuple-element.14.refs_0_, f32[64,128]{1,0:T(8,128)} %get-tuple-element.8.refs_1_, f32[64,1]{1,0:T(8,128)} %copy.19.off.refs_2_, f32[64,128]{1,0:T(8,128)} %pad.4.refs_3_), custom_call_target="tpu_custom_call" | custom-call | tf_op jit(solution)/shard_map/krylov/pallas_call | solution.py:388
  137.2 0.9 reshape.28
  138.1 0.7 copy.22
  138.8 0.9 reshape.29
  139.7 0.7 copy.23
  (1 shorter events, 0.0 us)
Async XLA Ops:
  8.7 11.5 %copy-start.2 = (s32[64]{0:T(128)S(1)}, s32[64]{0:T(128)}, u32[]{:S(2)}) copy-start(s32[64]{0:T(128)} %param.16) | copy-start | bytes 772
  8.7 12.2 %copy-start.1 = (f32[512,8]{0,1:T(8,128)S(1)}, f32[512,8]{0,1:T(8,128)}, u32[]{:S(2)}) copy-start(f32[512,8]{0,1:T(8,128)} %param.17) | copy-start | bytes 49156
  8.7 36.3 %all-to-all-start = ((f32[128,24,128]{2,1,0:T(8,128)}), f32[128,24,128]{2,1,0:T(8,128)S(1)}, u32[]{:S(2)}, u32[]{:S(2)}) async-start(f32[128,24,128]{2,1,0:T(8,128)} %fit_place.1), calls=%async_computation | async-start | bytes 3145728 | tf_op jit(solution)/shard_map/all_to_all | solution.py:361
  45.1 1.2 copy-start

commit v2 on v1

--- a/solution.py
+++ b/solution.py
@@ -20,6 +20,7 @@
 TRACKS = 512
 DEV = 128
 GROUP = 16
+PLACED = 32
 EPS = 1e-6
 MESH = pl.DeviceIdType.MESH
 CONTRACT_LANES = (((1,), (1,)), ((), ()))
@@ -61,18 +62,24 @@
     road = tr[...]
     rel = lax.rem(hm[...] - NPAR * road + NMOD, NMOD).astype(F32)
     local_road = jnp.broadcast_to((road & (ROADS - 1)).astype(F32), (NHIT, TRACKS))
-    words = [gd[p] * root for p in range(NPAR)] + proj + [solved, rel, local_road]
-    for w, value in enumerate(words):
-        for c in range(TRACKS // LANE):
-            part = value[:, c * LANE : (c + 1) * LANE]
-            lay[c, pl.ds(w, 8, stride=16), :] = part[:8]
-            lay[c, pl.ds(LANE + w, 4, stride=16), :] = part[8:]
+    words = proj + [solved, rel, local_road]
+    for c in range(TRACKS // LANE):
+        at = slice(c * LANE, (c + 1) * LANE)
+        for i in range(NHIT):
+            lay[c, 16 * i : 16 * i + 8, :] = gd[i, :, at] * root[i : i + 1, at]
+        for w, value in enumerate(words):
+            lay[c, pl.ds(8 + w, 8, stride=16), :] = value[:8, at]
+            lay[c, pl.ds(LANE + 8 + w, 4, stride=16), :] = value[8:, at]
     whole = jnp.concatenate([lay[c] for c in range(TRACKS // LANE)], axis=1)
-    first_hi, first_lo = split(whole[:LANE])
     tail = whole[LANE:]
     none = jnp.zeros_like(tail)
-    left_hi, left_lo = split(jnp.concatenate([tail, none], axis=0))
-    right_hi, right_lo = split(jnp.concatenate([none, tail], axis=0))
+
+    def both(value):
+        return jnp.concatenate(split(value), axis=0)
+
+    first_w = both(whole[:LANE])
+    left_w = both(jnp.concatenate([tail, none], axis=0))
+    right_w = both(jnp.concatenate([none, tail], axis=0))
 
     owner = road >> 6
     mine = lax.broadcasted_iota(jnp.int32, (DEV, TRACKS), 0) == owner
@@ -87,27 +94,26 @@
     slot = owner * CAP + rank.astype(jnp.int32)
 
     def place(step, carry):
-        row = lax.broadcasted_iota(jnp.int32, (GROUP * CAP, TRACKS), 0) + step * (GROUP * CAP)
+        row = lax.broadcasted_iota(jnp.int32, (PLACED * CAP, TRACKS), 0) + step * (PLACED * CAP)
         chosen = jnp.where(row == slot, 1.0, 0.0)
-        pick = chosen.astype(BF16)
-        first = dot_t(pick, first_hi) + dot_t(pick, first_lo)
-        halves = chosen.reshape(GROUP, 2, 8, TRACKS)
-        low = halves[:, 0].reshape(LANE, TRACKS).astype(BF16)
-        high = halves[:, 1].reshape(LANE, TRACKS).astype(BF16)
-        last = dot_t(low, left_hi) + dot_t(low, left_lo) + dot_t(high, right_hi) + dot_t(high, right_lo)
-        at = pl.ds(pl.multiple_of(step * GROUP, GROUP), GROUP)
-        send[at, 0:16, :] = first.reshape(GROUP, CAP, LANE)
-        send[at, 16:24, :] = last.reshape(GROUP, 8, LANE)
+        halves = chosen.reshape(PLACED, 2, 8, TRACKS)
+        low = halves[:, 0].reshape(PLACED * 8, TRACKS).astype(BF16)
+        high = halves[:, 1].reshape(PLACED * 8, TRACKS).astype(BF16)
+        first = dot_t(chosen.astype(BF16), first_w)
+        last = dot_t(low, left_w) + dot_t(high, right_w)
+        at = pl.ds(pl.multiple_of(step * PLACED, PLACED), PLACED)
+        send[at, 0:16, :] = (first[:, :LANE] + first[:, LANE:]).reshape(PLACED, CAP, LANE)
+        send[at, 16:24, :] = (last[:, :LANE] + last[:, LANE:]).reshape(PLACED, 8, LANE)
         return carry
 
-    lax.fori_loop(0, DEV // GROUP, place, 0)
+    lax.fori_loop(0, DEV // PLACED, place, 0)
 
 
 def kernel_send(ld, gd, me, hw, hm, hc, tr, send, lay):
     fit_and_place(ld, gd, me, hw, hm, hc, tr, send, lay)
 
 
-def assemble(x, off, blocks, road_rhs, g_ref, x_ref, hot_ref, mix_ref, z_ref):
+def assemble(x, off, blocks, road_rhs, g_ref, t_ref, x_ref, hot_ref, mix_ref, z_ref):
     t0 = x[:, 0:8, :].reshape(LANE, LANE).T
     t1 = x[:, 8:16, :].reshape(LANE, LANE).T
     t2 = x[:, 16:24, :].reshape(LANE, LANE).T
@@ -134,6 +140,7 @@
             g = jnp.where(same, hits[i][0], g)
             a = jnp.where(same, hits[i][1], a)
         g_ref[8 * s : 8 * s + 8, :] = g
+        t_ref[8 * s : 8 * s + 8, :] = 2.0 * g - g.astype(BF16).astype(F32)
         x_ref[0, 8 * s : 8 * s + 8, :] = a[:, :LANE]
         x_ref[1, 8 * s : 8 * s + 8, :] = a[:, LANE:]
         sums.append(g * a[5:6])
@@ -156,28 +163,39 @@
             mix = mix - a_s[a : a + 1] * lines[a]
         mix_ref[...] = mix
         for u in range(ROAD):
-            z = g_ref[8 * u : 8 * u + 8, :] * mix_ref[u : u + 1, :]
+            z = t_ref[8 * u : 8 * u + 8, :] * mix_ref[u : u + 1, :]
             z_ref[8 * u : 8 * u + 8, :] = z
-        z_hi, z_lo = split(z_ref[...])
-        pair = jnp.concatenate([g_s, g_s], axis=0)
-        g_hi, g_lo = split(pair)
+        z_both = jnp.concatenate(split(z_ref[...]), axis=0)
+        g_hi = jnp.concatenate([g_s, g_s], axis=0).astype(BF16)
         hot = hot_ref[...].reshape(ROADS // 2, 16, wide)
-        left_hi = (hot * g_hi[None]).reshape(ROADS * NPAR, wide)
-        left_lo = (hot * g_lo[None]).reshape(ROADS * NPAR, wide)
-        out = dot_t(left_hi, z_hi) + dot_t(left_hi, z_lo) + dot_t(left_lo, z_hi)
-        blocks[:, at, :] += out.reshape(ROADS, NPAR, LANE)
+        left = (hot * g_hi[None]).reshape(ROADS * NPAR, wide)
+        out = dot_t(left, z_both)
+        blocks[:, at, :] += (out[:, :LANE] + out[:, LANE:]).reshape(ROADS, NPAR, LANE)
         return carry
 
-    lax.fori_loop(0, ROAD, slot_step, 0)
-
-
-def kernel_assemble(x, off, blocks, road_rhs, g_ref, x_ref, hot_ref, mix_ref, z_ref):
+    lax.fori_loop(0, ROAD, slot_step, 0, unroll=2)
+
+
+def symmetric(blocks):
+    def one(r, carry):
+        block = blocks[r]
+        blocks[r] = 0.5 * (block + block.T)
+        return carry
+
+    lax.fori_loop(0, ROADS, one, 0, unroll=4)
+
+
+def kernel_assemble(x, off, blocks, road_rhs, g_ref, t_ref, x_ref, hot_ref, mix_ref, z_ref):
     @pl.when(pl.program_id(0) == 0)
     def _():
         blocks[...] = jnp.zeros_like(blocks)
         road_rhs[...] = jnp.zeros_like(road_rhs)
 
-    assemble(x[...], off[...], blocks, road_rhs, g_ref, x_ref, hot_ref, mix_ref, z_ref)
+    assemble(x[...], off[...], blocks, road_rhs, g_ref, t_ref, x_ref, hot_ref, mix_ref, z_ref)
+
+    @pl.when(pl.program_id(0) == pl.num_programs(0) - 1)
+    def _():
+        symmetric(blocks)
 
 
 HALF = 64
@@ -357,7 +375,7 @@
         out_specs=VM,
         scratch_shapes=[pltpu.VMEM((4, 192, LANE), F32)],
         name="fit_place",
-    )(ld, gd, me, hw, hm, hc.reshape(1, TRACKS), tr.reshape(1, TRACKS))
+    )(ld, jnp.transpose(gd, (1, 0, 2)), me, hw, hm, hc.reshape(1, TRACKS), tr.reshape(1, TRACKS))
     recv = lax.all_to_all(send, ("trk", "mod"), split_axis=0, concat_axis=0, tiled=True)
     off = (rs % NPAR).astype(F32).reshape(ROADS, 1)
     blocks, road_rhs = pl.pallas_call(
@@ -376,6 +394,7 @@
             pl.BlockSpec((ROADS, LANE), lambda c: (0, 0)),
         ),
         scratch_shapes=[
+            pltpu.VMEM((LANE, 2 * LANE), F32),
             pltpu.VMEM((LANE, 2 * LANE), F32),
             pltpu.VMEM((2, LANE, LANE), F32),
             pltpu.VMEM((ROADS * NPAR, 2 * LANE), BF16),

time: 141 us -> 113 us (0.80)
  Pallas kernels: 97.3 us -> 71.4 us
  local copies, waits for them, and re-layouts: 7.66 us -> 5.91 us
    pallas_call x1, Pallas kernels: 57.6 us -> 33.3 us  [on_device(): pl.pallas_call(kernel_assemble, grid=(DEV // GROUP,), out_shape=(jax.Shap...]
    unnamed x10 -> x9, local copies, waits for them, and re-layouts: 4.45 us -> 2.7 us
    pallas_call x1, Pallas kernels: 6.34 us -> 4.7 us  [on_device(): pl.pallas_call(kernel_send, out_shape=jax.ShapeDtypeStruct((DEV, 24, LANE...]
where the time goes in v2:
time: 113 us
  Pallas kernels  71.4 us (63%)
  waiting for transfers between devices  23.2 us (21%)
  starting transfers between devices  11.5 us (10%)
  local copies, waits for them, and re-layouts  5.91 us (5%)
    pallas_call x1, Pallas kernels, on_device(): pl.pallas_call(kernel_krylov, out_shape=(jax.ShapeDtypeStruct((HALF, LANE...  33.4 us
    pallas_call x1, Pallas kernels, on_device(): pl.pallas_call(kernel_assemble, grid=(DEV // GROUP,), out_shape=(jax.Shap...  33.3 us
    all_to_all x1, waiting for transfers between devices, on_device(): lax.all_to_all(send, ('trk', 'mod'), split_axis=0, concat_axis=0, tiled=T...  23.2 us
    all_to_all x1, starting transfers between devices, on_device(): lax.all_to_all(send, ('trk', 'mod'), split_axis=0, concat_axis=0, tiled=T...  11.5 us
    pallas_call x1, Pallas kernels, on_device(): pl.pallas_call(kernel_send, out_shape=jax.ShapeDtypeStruct((DEV, 24, LANE...  4.7 us
    unnamed x9, local copies, waits for them, and re-layouts  2.7 us
  transfers between devices with their start and end apart: 1, of which 1 were waited for; matrix products, arithmetic and copies ran while one was open for 1% of the time, Pallas kernels for 0%

profile of v2, /device:TPU:1, one launch (start us, length us, event | category | flops | bytes accessed | tf_op | source)
XLA Modules:
  0.0 112.7 jit_solution(5773963523356962303)
XLA Ops:
  0.6 4.7 %fit_place.1 = f32[128,24,128]{2,1,0:T(8,128)} custom-call(f32[5,12,512]{2,1,0:T(8,128)} %ld.1, f32[12,8,512]{2,1,0:T(8,128)} %bitcast.7, f32[12,512]{1,0:T(8,128)} %me.1, f32[12,512]{1,0:T(8,128)} %hw.1, s32[12,512]{1,0:T(8,128)} %hm.1, s32[1,512]{1,0:T(1,128)} %bitcast.10, s32[1,512]{1,0:T(1,128)} %bitcast.11), custom_call_target="tpu_custom_call" | custom-call | tf_op jit(solution)/shard_map/fit_place/pallas_call | solution.py:371
  5.3 0.0 copy-start.2
  5.3 0.0 copy-start.1
  5.3 11.5 %all-to-all-start = ((f32[128,24,128]{2,1,0:T(8,128)}), f32[128,24,128]{2,1,0:T(8,128)S(1)}, u32[]{:S(2)}, u32[]{:S(2)}) async-start(f32[128,24,128]{2,1,0:T(8,128)} %fit_place.1), calls=%async_computation | async-start | bytes 3145728 | tf_op jit(solution)/shard_map/all_to_all | solution.py:379
  16.8 0.0 copy-done.2
  16.8 0.7 copy.17.off.refs_2_
  17.5 0.0 copy-done.1
  17.5 0.1 copy.18
  17.7 0.1 reshape.27
  17.8 0.6 pad.4.refs_3_
  18.4 23.2 %all-to-all-done.x = f32[128,24,128]{2,1,0:T(8,128)S(1)} async-done(((f32[128,24,128]{2,1,0:T(8,128)}), f32[128,24,128]{2,1,0:T(8,128)S(1)}, u32[]{:S(2)}, u32[]{:S(2)}) %all-to-all-start) | async-done | bytes 1572896 | tf_op jit(solution)/shard_map/all_to_all | solution.py:379
  41.7 0.0 copy-start
  41.7 1.2 %copy-done = f32[128,24,128]{2,1,0:T(8,128)} copy-done((f32[128,24,128]{2,1,0:T(8,128)}, f32[128,24,128]{2,1,0:T(8,128)S(1)}, u32[]{:S(2)}) %copy-start) | copy-done | bytes 1572888
  42.8 33.3 %assemble.1 = (f32[64,128,128]{2,1,0:T(8,128)}, f32[64,128]{1,0:T(8,128)}) custom-call(f32[128,24,128]{2,1,0:T(8,128)} %copy-done, f32[64,1]{1,0:T(8,128)} %copy.17.off.refs_2_), custom_call_target="tpu_custom_call" | custom-call | tf_op jit(solution)/shard_map/assemble/pallas_call | solution.py:381
  76.1 33.4 %krylov.1 = (f32[64,128]{1,0:T(8,128)}, f32[64,128]{1,0:T(8,128)}) custom-call(f32[64,128,128]{2,1,0:T(8,128)} %get-tuple-element.14.refs_0_, f32[64,128]{1,0:T(8,128)} %get-tuple-element.8.refs_1_, f32[64,1]{1,0:T(8,128)} %copy.17.off.refs_2_, f32[64,128]{1,0:T(8,128)} %pad.4.refs_3_), custom_call_target="tpu_custom_call" | custom-call | tf_op jit(solution)/shard_map/krylov/pallas_call | solution.py:407
  109.5 0.9 reshape.28
  110.4 0.7 copy.20
  111.1 0.9 reshape.29
  112.0 0.7 copy.21
  (1 shorter events, 0.0 us)
Async XLA Ops:
  5.3 11.5 %copy-start.2 = (s32[64]{0:T(128)S(1)}, s32[64]{0:T(128)}, u32[]{:S(2)}) copy-start(s32[64]{0:T(128)} %param.16) | copy-start | bytes 772
  5.3 12.2 %copy-start.1 = (f32[512,8]{0,1:T(8,128)S(1)}, f32[512,8]{0,1:T(8,128)}, u32[]{:S(2)}) copy-start(f32[512,8]{0,1:T(8,128)} %param.17) | copy-start | bytes 49156
  5.3 36.3 %all-to-all-start = ((f32[128,24,128]{2,1,0:T(8,128)}), f32[128,24,128]{2,1,0:T(8,128)S(1)}, u32[]{:S(2)}, u32[]{:S(2)}) async-start(f32[128,24,128]{2,1,0:T(8,128)} %fit_place.1), calls=%async_computation | async-start | bytes 3145728 | tf_op jit(solution)/shard_map/all_to_all | solution.py:379
  41.7 1.2 %copy-start = (f32[128,24,128]{2,1,0:T(8,128)}, f32[128,24,128]{2,1,0:T(8,128)S(1)}, u32[]{:S(2)}) copy-start(f32[128,24,128]{2,1,0:T(8,128)S(1)} %all-to-all-done.x) | copy-start | bytes 4718596

commit v3 on v2

--- a/solution.py
+++ b/solution.py
@@ -107,10 +107,6 @@
         return carry
 
     lax.fori_loop(0, DEV // PLACED, place, 0)
-
-
-def kernel_send(ld, gd, me, hw, hm, hc, tr, send, lay):
-    fit_and_place(ld, gd, me, hw, hm, hc, tr, send, lay)
 
 
 def assemble(x, off, blocks, road_rhs, g_ref, t_ref, x_ref, hot_ref, mix_ref, z_ref):
@@ -185,19 +181,6 @@
     lax.fori_loop(0, ROADS, one, 0, unroll=4)
 
 
-def kernel_assemble(x, off, blocks, road_rhs, g_ref, t_ref, x_ref, hot_ref, mix_ref, z_ref):
-    @pl.when(pl.program_id(0) == 0)
-    def _():
-        blocks[...] = jnp.zeros_like(blocks)
-        road_rhs[...] = jnp.zeros_like(road_rhs)
-
-    assemble(x[...], off[...], blocks, road_rhs, g_ref, t_ref, x_ref, hot_ref, mix_ref, z_ref)
-
-    @pl.when(pl.program_id(0) == pl.num_programs(0) - 1)
-    def _():
-        symmetric(blocks)
-
-
 HALF = 64
 
 
@@ -230,50 +213,131 @@
     return jnp.sum(jnp.sum(x, axis=0, keepdims=True), axis=1, keepdims=True)
 
 
-def krylov(blocks, road_rhs, off, prior, rhs_out, cor_out, field, vec, image, mapped, up, down,
-           from_prev, from_next, line, lines, sems, gsem):
-    trk, mod = lax.axis_index("trk"), lax.axis_index("mod")
+def to_rows(x, flat):
+    for c in range(TRACKS // LANE):
+        block = jnp.concatenate([x[:, c * LANE : (c + 1) * LANE], jnp.zeros((LANE - NPAR, LANE), F32)], axis=0)
+        flat[c * LANE : (c + 1) * LANE, :] = block.T
+    rows = flat[pl.ds(0, HALF, stride=8), :]
+    for m in range(1, NPAR):
+        rows = rows + pltpu.roll(flat[pl.ds(m, HALF, stride=8), :], 8 * m, 1)
+    return rows
+
+
+def from_rows(rows, flat):
+    flat[pl.ds(0, HALF, stride=8), :] = rows
+    for m in range(1, NPAR):
+        flat[pl.ds(m, HALF, stride=8), :] = pltpu.roll(rows, LANE - 8 * m, 1)
+    return jnp.concatenate(
+        [flat[c * LANE : (c + 1) * LANE, :].T[:NPAR] for c in range(TRACKS // LANE)], axis=1
+    )
+
+
+def position():
+    return lax.axis_index("trk"), lax.axis_index("mod")
+
+
+def place_of(d):
+    return (d // 8, lax.rem(d, 8))
+
+
+def chunk_target(n, trk, mod):
+    c, j = n // GROUP, lax.rem(n, GROUP)
+    m = lax.rem(c + j, 8)
+    z, y = lax.rem(trk // 4 + j // 4, 4), lax.rem(lax.rem(trk, 4) + lax.rem(j, 4), 4)
+    x, core = lax.rem(mod // 2 + m // 2, 4), lax.rem(mod + m, 2)
+    return z * 4 + y, x * 2 + core
+
+
+def kernel_all(ld, gd, me_ref, hw, hm, hc, tr, rs, pw, blocks_out, rhs_out, cor_out,
+               send, recv, lay, blocks, road_rhs, g_ref, t_ref, x_ref, hot_ref, mix_ref, z_ref,
+               field, vec, mapped, prior, flat, up, down, from_prev, from_next, line, lines,
+               send_sem, recv_sem, rim_sem, line_sem, out_sem):
+    trk, mod = position()
     me = trk * 8 + mod
+    barrier = pltpu.get_barrier_semaphore()
+
+    def greet(k, carry):
+        pl.semaphore_signal(barrier, inc=1, device_id=place_of(lax.rem(me + k, DEV)), device_id_type=MESH)
+        return carry
+
+    lax.fori_loop(1, DEV, greet, 0)
+    fit_and_place(ld, gd, me_ref, hw, hm, hc, tr, send, lay)
+    pl.semaphore_wait(barrier, DEV - 1)
+
+    own = pltpu.make_async_copy(send.at[me], recv.at[0], recv_sem.at[0])
+    own.start()
+
+    def send_chunk(n, carry):
+        t, m = chunk_target(n, trk, mod)
+        pltpu.make_async_remote_copy(
+            send.at[t * 8 + m], recv.at[n], send_sem, recv_sem.at[n // GROUP], device_id=(t, m), device_id_type=MESH
+        ).start()
+        return carry
+
+    lax.fori_loop(1, DEV, send_chunk, 0)
+
+    start = lax.rem(rs[...], NPAR).astype(F32)
+    diagonal = lax.broadcasted_iota(jnp.int32, (ROADS, ROADS), 0) == lax.broadcasted_iota(
+        jnp.int32, (ROADS, ROADS), 1
+    )
+    off = jnp.sum(jnp.where(diagonal, start, 0.0), axis=1, keepdims=True)
+    prior[...] = to_rows(pw[...], flat)
+    blocks[...] = jnp.zeros_like(blocks)
+    road_rhs[...] = jnp.zeros_like(road_rhs)
+
+    def take_group(c, carry):
+        at = pl.ds(pl.multiple_of(c * GROUP, GROUP), GROUP)
+        pltpu.make_async_copy(recv.at[at], recv.at[at], recv_sem.at[c]).wait()
+        assemble(recv[at], off, blocks, road_rhs, g_ref, t_ref, x_ref, hot_ref, mix_ref, z_ref)
+        return carry
+
+    lax.fori_loop(0, DEV // GROUP, take_group, 0)
+
     nxt = lax.rem(me + 1, DEV)
     prv = lax.rem(me + DEV - 1, DEV)
-    off = off[...]
-
-    def place(d):
-        return (d // 8, lax.rem(d, 8))
-
-    def exchange(e, target):
+    out_copy = pltpu.make_async_copy(blocks, blocks_out, out_sem)
+
+    def exchange(e, target, between):
         up[e] = field[64:72, :]
         down[e] = field[0:8, :]
         to_next = pltpu.make_async_remote_copy(
-            up.at[e], from_prev.at[e], sems.at[e, 0], sems.at[e, 1], device_id=place(nxt), device_id_type=MESH
+            up.at[e], from_prev.at[e], rim_sem.at[e, 0], rim_sem.at[e, 1], device_id=place_of(nxt), device_id_type=MESH
         )
         to_prev = pltpu.make_async_remote_copy(
-            down.at[e], from_next.at[e], sems.at[e, 2], sems.at[e, 3], device_id=place(prv), device_id_type=MESH
+            down.at[e], from_next.at[e], rim_sem.at[e, 2], rim_sem.at[e, 3], device_id=place_of(prv), device_id_type=MESH
         )
         to_next.start()
         to_prev.start()
         target[8:64, :] = field[8:64, :]
+        between()
         to_next.wait()
         to_prev.wait()
         keep = lax.broadcasted_iota(jnp.int32, (8, LANE), 0) < 2
         target[0:8, :] = field[0:8, :] + jnp.where(keep, from_prev[e], 0.0)
         target[64:72, :] = jnp.where(keep, field[64:72, :] + from_next[e], 0.0)
 
-    def apply(source, e, target):
-        piece = gather(source, off)
-        flipped = piece.T
+    def apply(source, e, target, between):
+        flipped = gather(source, off).T
         for r in range(ROADS):
-            row = jnp.sum(blocks[r] * flipped[:, r : r + 1], axis=0, keepdims=True)
-            mapped[r : r + 1, :] = row
+            mapped[r : r + 1, :] = jnp.sum(blocks[r] * flipped[:, r : r + 1], axis=0, keepdims=True)
         spread(mapped[...], off, field)
         field[0:64, :] += prior[...] * source[0:64, :]
-        exchange(e, target)
+        exchange(e, target, between)
+
+    def finish_blocks():
+        symmetric(blocks)
+        out_copy.start()
+
+    def give_rhs():
+        rhs_out[...] = from_rows(vec[0, 0:64, :], flat)
+
+    def nothing():
+        pass
 
     spread(road_rhs[...], off, field)
-    exchange(0, vec.at[0])
-    rhs_out[...] = vec[0, 0:64, :]
-    apply(vec.at[0], 1, vec.at[1])
-    apply(vec.at[1], 2, vec.at[2])
+    exchange(0, vec.at[0], finish_blocks)
+    apply(vec.at[0], 1, vec.at[1], give_rhs)
+    apply(vec.at[1], 2, vec.at[2], nothing)
     b, w, u = vec[0, 0:64, :], vec[1, 0:64, :], vec[2, 0:64, :]
 
     def unit(norm):
@@ -298,16 +362,17 @@
     lines[me] = row
 
     def send_line(k, carry):
-        other = lax.rem(me + k, DEV)
         pltpu.make_async_remote_copy(
-            line, lines.at[me], gsem.at[0], gsem.at[1], device_id=place(other), device_id_type=MESH
+            line, lines.at[me], line_sem.at[0], line_sem.at[1],
+            device_id=place_of(lax.rem(me + k, DEV)), device_id_type=MESH,
         ).start()
         return carry
 
     lax.fori_loop(1, DEV, send_line, 0)
+    w8 = from_rows(w, flat)
     whole = pltpu.make_async_remote_copy(
-        lines.at[pl.ds(0, DEV - 1)], lines.at[pl.ds(0, DEV - 1)], gsem.at[0], gsem.at[1],
-        device_id=place(nxt), device_id_type=MESH,
+        lines.at[pl.ds(0, DEV - 1)], lines.at[pl.ds(0, DEV - 1)], line_sem.at[0], line_sem.at[1],
+        device_id=place_of(nxt), device_id_type=MESH,
     )
     whole.wait_recv()
     every = lines[...]
@@ -341,96 +406,77 @@
     determinant = first * second - cross * cross
     coef_one = beta_one * (second * alpha_one - cross * beta_two) / determinant
     coef_two = beta_one * (first * beta_two - cross * alpha_one) / determinant
-    v1 = b * inv_one
-    v2 = (w * inv_one - alpha_one * v1) * inv_two
+    v1 = rhs_out[...] * inv_one
+    v2 = (w8 * inv_one - alpha_one * v1) * inv_two
     cor_out[...] = coef_one * v1 + coef_two * v2
     whole.wait_send()
-
-
-def kernel_krylov(*refs):
-    trk, mod = lax.axis_index("trk"), lax.axis_index("mod")
-    me = trk * 8 + mod
-    barrier = pltpu.get_barrier_semaphore()
-
-    def greet(k, carry):
-        other = lax.rem(me + k, DEV)
-        pl.semaphore_signal(
-            barrier, inc=1, device_id=(other // 8, lax.rem(other, 8)), device_id_type=MESH
-        )
-        return carry
-
-    lax.fori_loop(1, DEV, greet, 0)
-    pl.semaphore_wait(barrier, DEV - 1)
-    krylov(*refs)
+    sent = pltpu.make_async_remote_copy(
+        send.at[pl.ds(0, DEV - 1)], recv.at[pl.ds(0, DEV - 1)], send_sem, recv_sem.at[0],
+        device_id=place_of(nxt), device_id_type=MESH,
+    )
+    sent.wait_send()
+    out_copy.wait()
 
 
 VM = pl.BlockSpec(memory_space=pltpu.VMEM)
 
 
 def on_device(ld, gd, me, hw, hm, hc, tr, rs, pw):
-    send = pl.pallas_call(
-        kernel_send,
-        out_shape=jax.ShapeDtypeStruct((DEV, 24, LANE), F32),
-        in_specs=[VM] * 7,
-        out_specs=VM,
-        scratch_shapes=[pltpu.VMEM((4, 192, LANE), F32)],
-        name="fit_place",
-    )(ld, jnp.transpose(gd, (1, 0, 2)), me, hw, hm, hc.reshape(1, TRACKS), tr.reshape(1, TRACKS))
-    recv = lax.all_to_all(send, ("trk", "mod"), split_axis=0, concat_axis=0, tiled=True)
-    off = (rs % NPAR).astype(F32).reshape(ROADS, 1)
-    blocks, road_rhs = pl.pallas_call(
-        kernel_assemble,
-        grid=(DEV // GROUP,),
+    def vmem(*shape, dtype=F32):
+        return pltpu.VMEM(shape, dtype)
+
+    blocks, rhs, cor = pl.pallas_call(
+        kernel_all,
         out_shape=(
             jax.ShapeDtypeStruct((ROADS, LANE, LANE), F32),
-            jax.ShapeDtypeStruct((ROADS, LANE), F32),
+            jax.ShapeDtypeStruct((NPAR, TRACKS), F32),
+            jax.ShapeDtypeStruct((NPAR, TRACKS), F32),
         ),
-        in_specs=[
-            pl.BlockSpec((GROUP, 24, LANE), lambda c: (c, 0, 0)),
-            pl.BlockSpec((ROADS, 1), lambda c: (0, 0)),
-        ],
-        out_specs=(
-            pl.BlockSpec((ROADS, LANE, LANE), lambda c: (0, 0, 0)),
-            pl.BlockSpec((ROADS, LANE), lambda c: (0, 0)),
-        ),
+        in_specs=[VM] * 9,
+        out_specs=(pl.BlockSpec(memory_space=pl.ANY), VM, VM),
         scratch_shapes=[
-            pltpu.VMEM((LANE, 2 * LANE), F32),
-            pltpu.VMEM((LANE, 2 * LANE), F32),
-            pltpu.VMEM((2, LANE, LANE), F32),
-            pltpu.VMEM((ROADS * NPAR, 2 * LANE), BF16),
-            pltpu.VMEM((ROAD, 2 * LANE), F32),
-            pltpu.VMEM((LANE, 2 * LANE), F32),
-        ],
-        name="assemble",
-    )(recv, off)
-    prior = jnp.pad(pw.reshape(HALF, HALF), ((0, 0), (0, HALF)))
-    rhs, cor = pl.pallas_call(
-        kernel_krylov,
-        out_shape=(jax.ShapeDtypeStruct((HALF, LANE), F32), jax.ShapeDtypeStruct((HALF, LANE), F32)),
-        in_specs=[VM] * 4,
-        out_specs=(VM, VM),
-        scratch_shapes=[
-            pltpu.VMEM((72, LANE), F32),
-            pltpu.VMEM((3, 72, LANE), F32),
-            pltpu.VMEM((72, LANE), F32),
-            pltpu.VMEM((ROADS, LANE), F32),
-            pltpu.VMEM((3, 8, LANE), F32),
-            pltpu.VMEM((3, 8, LANE), F32),
-            pltpu.VMEM((3, 8, LANE), F32),
-            pltpu.VMEM((3, 8, LANE), F32),
-            pltpu.VMEM((1, LANE), F32),
-            pltpu.VMEM((DEV, 1, LANE), F32),
+            vmem(DEV, 24, LANE),
+            vmem(DEV, 24, LANE),
+            vmem(4, 192, LANE),
+            vmem(ROADS, LANE, LANE),
+            vmem(ROADS, LANE),
+            vmem(LANE, 2 * LANE),
+            vmem(LANE, 2 * LANE),
+            vmem(2, LANE, LANE),
+            vmem(ROADS * NPAR, 2 * LANE, dtype=BF16),
+            vmem(ROAD, 2 * LANE),
+            vmem(LANE, 2 * LANE),
+            vmem(72, LANE),
+            vmem(3, 72, LANE),
+            vmem(ROADS, LANE),
+            vmem(HALF, LANE),
+            vmem(TRACKS, LANE),
+            vmem(3, 8, LANE),
+            vmem(3, 8, LANE),
+            vmem(3, 8, LANE),
+            vmem(3, 8, LANE),
+            vmem(1, LANE),
+            vmem(DEV, 1, LANE),
+            pltpu.SemaphoreType.DMA,
+            pltpu.SemaphoreType.DMA((DEV // GROUP,)),
             pltpu.SemaphoreType.DMA((3, 4)),
             pltpu.SemaphoreType.DMA((2,)),
+            pltpu.SemaphoreType.DMA,
         ],
         compiler_params=pltpu.CompilerParams(collective_id=0, has_side_effects=True),
-        name="krylov",
-    )(blocks, road_rhs, off, prior)
-    return (
-        blocks,
-        rhs[:, :HALF].reshape(TRACKS, NPAR),
-        cor[:, :HALF].reshape(TRACKS, NPAR),
-    )
+        name="alignment",
+    )(
+        ld,
+        jnp.transpose(gd, (1, 0, 2)),
+        me,
+        hw,
+        hm,
+        hc.reshape(1, TRACKS),
+        tr.reshape(1, TRACKS),
+        rs.reshape(1, ROADS),
+        pw.T,
+    )
+    return blocks, rhs.T, cor.T
 
 
 def solution(mesh):

time: 113 us -> 81.1 us (0.72)
  waiting for transfers between devices: 23.2 us -> 0 us
  starting transfers between devices: 11.5 us -> 0 us
  Pallas kernels: 71.4 us -> 74.3 us
    all_to_all x1 -> x0, waiting for transfers between devices: 23.2 us -> none  [on_device(): lax.all_to_all(send, ('trk', 'mod'), split_axis=0, concat_axis=0, tiled=T...]
    all_to_all x1 -> x0, starting transfers between devices: 11.5 us -> none  [on_device(): lax.all_to_all(send, ('trk', 'mod'), split_axis=0, concat_axis=0, tiled=T...]
    unnamed x9 -> x7, local copies, waits for them, and re-layouts: 2.7 us -> 5.93 us
    pallas_call x3 -> x1, Pallas kernels: 71.4 us -> 74.3 us  [on_device(): pl.pallas_call(kernel_all, out_shape=(jax.ShapeDtypeStruct((ROADS, LANE,...]
    reshape x4 -> x0, local copies, waits for them, and re-layouts: 2.59 us -> none  [the longest x1 0.88 us: on_device(): rhs[:, :HALF].reshape(TRACKS, NPAR)]
  transfers between devices with their start and end apart: 1 -> 0, of which waited for: 1 -> 0; matrix products, arithmetic and copies ran while one was open for 1% -> 0% of each run, Pallas kernels for 0% -> 0%
where the time goes in v3:
time: 81.1 us; the launch traced here: 80.9 us
  Pallas kernels  74.3 us (92%)
  local copies, waits for them, and re-layouts  5.93 us (7%)
    pallas_call x1, Pallas kernels, on_device(): pl.pallas_call(kernel_all, out_shape=(jax.ShapeDtypeStruct((ROADS, LANE,...  74.3 us
    unnamed x7, local copies, waits for them, and re-layouts  5.93 us

profile of v3, /device:TPU:1, one launch (start us, length us, event | category | flops | bytes accessed | tf_op | source)
XLA Modules:
  0.0 80.9 jit_solution(314332693747951150)
XLA Ops:
  0.6 74.3 %alignment.1 = (f32[64,128,128]{2,1,0:T(8,128)}, f32[8,512]{1,0:T(8,128)}, f32[8,512]{1,0:T(8,128)}) custom-call(f32[5,12,512]{2,1,0:T(8,128)} %ld.1, f32[12,8,512]{2,1,0:T(8,128)} %bitcast.7, f32[12,512]{1,0:T(8,128)} %me_ref.1, f32[12,512]{1,0:T(8,128)} %hw.1, s32[12,512]{1,0:T(8,128)} %hm.1, s32[1,512]{1,0:T(1,128)} %bitcast.11, s32[1,512]{1,0:T(1,128)} %bitcast.12, ...), custom_call_target="tpu_custom_call" | custom-call | tf_op jit(solution)/shard_map/alignment/pallas_call | solution.py:428
  75.0 0.0 copy-start.1
  75.0 0.0 copy-start
  75.0 4.7 %copy.15 = f32[64,128,128]{2,1,0:T(8,128)} copy(f32[64,128,128]{2,1,0:T(8,128)} %get-tuple-element.12) | data formatting | bytes 8388608
  79.7 0.0 copy-done.1
  79.7 0.6 copy.16
  80.3 0.0 copy-done
  80.3 0.6 copy.17
Async XLA Ops:
  75.0 4.7 %copy-start.1 = (f32[8,512]{1,0:T(8,128)S(1)}, f32[8,512]{1,0:T(8,128)}, u32[]{:S(2)}) copy-start(f32[8,512]{1,0:T(8,128)} %get-tuple-element.7) | copy-start | bytes 49156
  75.0 5.3 %copy-start = (f32[8,512]{1,0:T(8,128)S(1)}, f32[8,512]{1,0:T(8,128)}, u32[]{:S(2)}) copy-start(f32[8,512]{1,0:T(8,128)} %get-tuple-element.8) | copy-start | bytes 49156

commit v4 on v3

--- a/solution.py
+++ b/solution.py
@@ -35,7 +35,7 @@
     return hi, (x - hi.astype(F32)).astype(BF16)
 
 
-def fit_and_place(ld, gd, me, hw, hm, hc, tr, send, lay):
+def fit_and_place(ld, gd, me, hw, hm, hc, tr, send, lay, trk, mod, ready):
     position = lax.broadcasted_iota(jnp.int32, (NHIT, TRACKS), 0)
     live = position < hc[...]
     root = jnp.where(live, jnp.sqrt(hw[...]), 0.0)
@@ -82,8 +82,11 @@
     right_w = both(jnp.concatenate([none, tail], axis=0))
 
     owner = road >> 6
-    mine = lax.broadcasted_iota(jnp.int32, (DEV, TRACKS), 0) == owner
-    member = jnp.where(mine, 1.0, 0.0)
+    z, y, x, core = trk // 4, lax.rem(trk, 4), mod // 2, lax.rem(mod, 2)
+    j = (((owner >> 5) - z) & 3) * 4 + (((owner >> 3) - y) & 3)
+    m = (((owner >> 1) - x) & 3) * 2 + ((owner - core) & 1)
+    chunk = ((m - j) & 7) * GROUP + j
+    member = jnp.where(lax.broadcasted_iota(jnp.int32, (DEV, TRACKS), 0) == chunk, 1.0, 0.0)
     earlier = lax.broadcasted_iota(jnp.int32, (TRACKS, TRACKS), 0) <= lax.broadcasted_iota(
         jnp.int32, (TRACKS, TRACKS), 1
     )
@@ -91,9 +94,9 @@
         member.astype(BF16), jnp.where(earlier, 1.0, 0.0).astype(BF16), preferred_element_type=F32
     )
     rank = jnp.sum(member * running, axis=0, keepdims=True) - 1.0
-    slot = owner * CAP + rank.astype(jnp.int32)
-
-    def place(step, carry):
+    slot = chunk * CAP + rank.astype(jnp.int32)
+
+    for step in range(DEV // PLACED):
         row = lax.broadcasted_iota(jnp.int32, (PLACED * CAP, TRACKS), 0) + step * (PLACED * CAP)
         chosen = jnp.where(row == slot, 1.0, 0.0)
         halves = chosen.reshape(PLACED, 2, 8, TRACKS)
@@ -101,15 +104,13 @@
         high = halves[:, 1].reshape(PLACED * 8, TRACKS).astype(BF16)
         first = dot_t(chosen.astype(BF16), first_w)
         last = dot_t(low, left_w) + dot_t(high, right_w)
-        at = pl.ds(pl.multiple_of(step * PLACED, PLACED), PLACED)
+        at = slice(step * PLACED, (step + 1) * PLACED)
         send[at, 0:16, :] = (first[:, :LANE] + first[:, LANE:]).reshape(PLACED, CAP, LANE)
         send[at, 16:24, :] = (last[:, :LANE] + last[:, LANE:]).reshape(PLACED, 8, LANE)
-        return carry
-
-    lax.fori_loop(0, DEV // PLACED, place, 0)
-
-
-def assemble(x, off, blocks, road_rhs, g_ref, t_ref, x_ref, hot_ref, mix_ref, z_ref):
+        ready(step)
+
+
+def assemble(x, off, blocks, road_rhs, g_ref, t_ref, x_ref, hot_ref, mix_ref):
     t0 = x[:, 0:8, :].reshape(LANE, LANE).T
     t1 = x[:, 8:16, :].reshape(LANE, LANE).T
     t2 = x[:, 16:24, :].reshape(LANE, LANE).T
@@ -150,26 +151,29 @@
         for a in range(NLOC)
     ]
 
-    def slot_step(s, carry):
-        at = pl.ds(pl.multiple_of(s * 8, 8), 8)
+    ident = lax.broadcasted_iota(jnp.int32, (ROAD, wide), 0)
+    for s in range(ROAD):
+        mix = jnp.where(ident == s, 1.0, 0.0)
+        for a in range(NLOC):
+            mix = mix - lines[a][s : s + 1] * lines[a]
+        mix_ref[ROAD * s : ROAD * s + ROAD, :] = mix
+
+    for s in range(ROAD):
+        at = slice(8 * s, 8 * s + 8)
+        z = jnp.concatenate(
+            [
+                t_ref[8 * u : 8 * u + 8, :] * mix_ref[ROAD * s + u : ROAD * s + u + 1, :]
+                for u in range(ROAD)
+            ],
+            axis=0,
+        )
+        z_both = jnp.concatenate(split(z), axis=0)
         g_s = g_ref[at, :]
-        a_s = jnp.concatenate([x_ref[0, at, :], x_ref[1, at, :]], axis=1)
-        mix = jnp.where(lax.broadcasted_iota(jnp.int32, (ROAD, wide), 0) == s, 1.0, 0.0)
-        for a in range(NLOC):
-            mix = mix - a_s[a : a + 1] * lines[a]
-        mix_ref[...] = mix
-        for u in range(ROAD):
-            z = t_ref[8 * u : 8 * u + 8, :] * mix_ref[u : u + 1, :]
-            z_ref[8 * u : 8 * u + 8, :] = z
-        z_both = jnp.concatenate(split(z_ref[...]), axis=0)
         g_hi = jnp.concatenate([g_s, g_s], axis=0).astype(BF16)
         hot = hot_ref[...].reshape(ROADS // 2, 16, wide)
         left = (hot * g_hi[None]).reshape(ROADS * NPAR, wide)
         out = dot_t(left, z_both)
         blocks[:, at, :] += (out[:, :LANE] + out[:, LANE:]).reshape(ROADS, NPAR, LANE)
-        return carry
-
-    lax.fori_loop(0, ROAD, slot_step, 0, unroll=2)
 
 
 def symmetric(blocks):
@@ -240,41 +244,38 @@
     return (d // 8, lax.rem(d, 8))
 
 
-def chunk_target(n, trk, mod):
-    c, j = n // GROUP, lax.rem(n, GROUP)
-    m = lax.rem(c + j, 8)
-    z, y = lax.rem(trk // 4 + j // 4, 4), lax.rem(lax.rem(trk, 4) + lax.rem(j, 4), 4)
-    x, core = lax.rem(mod // 2 + m // 2, 4), lax.rem(mod + m, 2)
-    return z * 4 + y, x * 2 + core
-
-
 def kernel_all(ld, gd, me_ref, hw, hm, hc, tr, rs, pw, blocks_out, rhs_out, cor_out,
-               send, recv, lay, blocks, road_rhs, g_ref, t_ref, x_ref, hot_ref, mix_ref, z_ref,
+               send, recv, lay, blocks, road_rhs, g_ref, t_ref, x_ref, hot_ref, mix_ref,
                field, vec, mapped, prior, flat, up, down, from_prev, from_next, line, lines,
                send_sem, recv_sem, rim_sem, line_sem, out_sem):
     trk, mod = position()
     me = trk * 8 + mod
     barrier = pltpu.get_barrier_semaphore()
 
-    def greet(k, carry):
-        pl.semaphore_signal(barrier, inc=1, device_id=place_of(lax.rem(me + k, DEV)), device_id_type=MESH)
-        return carry
-
-    lax.fori_loop(1, DEV, greet, 0)
-    fit_and_place(ld, gd, me_ref, hw, hm, hc, tr, send, lay)
-    pl.semaphore_wait(barrier, DEV - 1)
-
-    own = pltpu.make_async_copy(send.at[me], recv.at[0], recv_sem.at[0])
-    own.start()
-
-    def send_chunk(n, carry):
-        t, m = chunk_target(n, trk, mod)
-        pltpu.make_async_remote_copy(
-            send.at[t * 8 + m], recv.at[n], send_sem, recv_sem.at[n // GROUP], device_id=(t, m), device_id_type=MESH
-        ).start()
-        return carry
-
-    lax.fori_loop(1, DEV, send_chunk, 0)
+    z, y, x, core = trk // 4, lax.rem(trk, 4), mod // 2, lax.rem(mod, 2)
+    zs = [lax.rem(z + d, 4) * 4 for d in range(4)]
+    ys = [lax.rem(y + d, 4) for d in range(4)]
+    xs = [lax.rem(x + d, 4) * 2 for d in range(4)]
+    cores = [core, 1 - core]
+    trks = [zs[j // 4] + ys[j % 4] for j in range(GROUP)]
+    mods = [xs[m // 2] + cores[m % 2] for m in range(8)]
+    others = [(trks[j], mods[m]) for m in range(8) for j in range(GROUP) if j or m]
+    for other in others:
+        pl.semaphore_signal(barrier, inc=1, device_id=other, device_id_type=MESH)
+    own = pltpu.make_async_copy(send.at[0], recv.at[0], recv_sem.at[0])
+
+    def ready(step):
+        if step == 0:
+            pl.semaphore_wait(barrier, DEV - 1)
+            own.start()
+        for n in range(max(1, step * PLACED), (step + 1) * PLACED):
+            c, j = n // GROUP, n % GROUP
+            pltpu.make_async_remote_copy(
+                send.at[n], recv.at[n], send_sem, recv_sem.at[c],
+                device_id=(trks[j], mods[(c + j) % 8]), device_id_type=MESH,
+            ).start()
+
+    fit_and_place(ld, gd, me_ref, hw, hm, hc, tr, send, lay, trk, mod, ready)
 
     start = lax.rem(rs[...], NPAR).astype(F32)
     diagonal = lax.broadcasted_iota(jnp.int32, (ROADS, ROADS), 0) == lax.broadcasted_iota(
@@ -288,7 +289,7 @@
     def take_group(c, carry):
         at = pl.ds(pl.multiple_of(c * GROUP, GROUP), GROUP)
         pltpu.make_async_copy(recv.at[at], recv.at[at], recv_sem.at[c]).wait()
-        assemble(recv[at], off, blocks, road_rhs, g_ref, t_ref, x_ref, hot_ref, mix_ref, z_ref)
+        assemble(recv[at], off, blocks, road_rhs, g_ref, t_ref, x_ref, hot_ref, mix_ref)
         return carry
 
     lax.fori_loop(0, DEV // GROUP, take_group, 0)
@@ -340,63 +341,53 @@
     apply(vec.at[1], 2, vec.at[2], nothing)
     b, w, u = vec[0, 0:64, :], vec[1, 0:64, :], vec[2, 0:64, :]
 
-    def unit(norm):
-        return jnp.where(norm > 0.0, 1.0 / jnp.where(norm > 0.0, norm, 1.0), 0.0)
-
-    r11 = jnp.sqrt(total(b * b))
-    q1 = b * unit(r11)
-    r12 = total(q1 * w)
-    r13 = total(q1 * u)
-    w1 = w - r12 * q1
-    u1 = u - r13 * q1
-    r22 = jnp.sqrt(total(w1 * w1))
-    q2 = w1 * unit(r22)
-    r23 = total(q2 * u1)
-    u2 = u1 - r23 * q2
-    r33 = jnp.sqrt(total(u2 * u2))
+    def inverse(value):
+        return jnp.where(value > 0.0, 1.0 / jnp.where(value > 0.0, value, 1.0), 0.0)
+
+    bb, bw, bu = total(b * b), total(b * w), total(b * u)
+    inv_bb = inverse(bb)
+    w1 = w - (bw * inv_bb) * b
+    u1 = u - (bu * inv_bb) * b
+    ww, wu = total(w1 * w1), total(w1 * u1)
+    u2 = u1 - (wu * inverse(ww)) * w1
+    uu = total(u2 * u2)
+    r11, r22 = jnp.sqrt(bb), jnp.sqrt(ww)
     lane = lax.broadcasted_iota(jnp.int32, (1, LANE), 1)
     row = jnp.zeros((1, LANE), F32)
-    for n, value in enumerate((r11, r12, r13, r22, r23, r33)):
+    for n, value in enumerate((r11, bw * inverse(r11), bu * inverse(r11), r22, wu * inverse(r22), jnp.sqrt(uu))):
         row = jnp.where(lane == n, value, row)
     line[...] = row
     lines[me] = row
-
-    def send_line(k, carry):
+    for other in others:
         pltpu.make_async_remote_copy(
-            line, lines.at[me], line_sem.at[0], line_sem.at[1],
-            device_id=place_of(lax.rem(me + k, DEV)), device_id_type=MESH,
+            line, lines.at[me], line_sem.at[0], line_sem.at[1], device_id=other, device_id_type=MESH
         ).start()
-        return carry
-
-    lax.fori_loop(1, DEV, send_line, 0)
     w8 = from_rows(w, flat)
     whole = pltpu.make_async_remote_copy(
         lines.at[pl.ds(0, DEV - 1)], lines.at[pl.ds(0, DEV - 1)], line_sem.at[0], line_sem.at[1],
         device_id=place_of(nxt), device_id_type=MESH,
     )
     whole.wait_recv()
-    every = lines[...]
-
-    def col(n):
-        return every[:, :, n : n + 1]
+    for d in range(DEV):
+        flat[d : d + 1, :] = lines[d]
+    every = flat[0:DEV, :].T
 
     def add(x):
-        return jnp.sum(x, axis=0)
-
-    b0, w0, u0, w1, u1, u2 = (col(n) for n in range(6))
-    beta_one = jnp.sqrt(add(b0 * b0) + EPS)
+        return jnp.sum(x, axis=1, keepdims=True)
+
+    b0, w0, u0, w1, u1, u2 = (every[n : n + 1, :] for n in range(6))
+    square = add(b0 * b0) + EPS
+    alpha_one = add(b0 * w0) / square
+    beta_one = jnp.sqrt(square)
     inv_one = 1.0 / beta_one
-    b0 = b0 * inv_one
-    w0, w1 = w0 * inv_one, w1 * inv_one
-    u0, u1, u2 = u0 * inv_one, u1 * inv_one, u2 * inv_one
-    alpha_one = add(b0 * w0)
-    x0, x1 = w0 - alpha_one * b0, w1
+    x0, x1 = (w0 - alpha_one * b0) * inv_one, w1 * inv_one
     beta_two = jnp.sqrt(add(x0 * x0 + x1 * x1) + EPS)
     inv_two = 1.0 / beta_two
     x0, x1 = x0 * inv_two, x1 * inv_two
-    y0 = (u0 - alpha_one * w0) * inv_two - beta_two * b0
-    y1 = (u1 - alpha_one * w1) * inv_two
-    y2 = u2 * inv_two
+    both_inv = inv_one * inv_two
+    y0 = (u0 - alpha_one * w0) * both_inv - beta_two * inv_one * b0
+    y1 = (u1 - alpha_one * w1) * both_inv
+    y2 = u2 * both_inv
     alpha_two = add(x0 * y0 + x1 * y1)
     y0, y1 = y0 - alpha_two * x0, y1 - alpha_two * x1
     beta_three = jnp.sqrt(add(y0 * y0 + y1 * y1 + y2 * y2) + EPS)
@@ -444,8 +435,7 @@
             vmem(LANE, 2 * LANE),
             vmem(2, LANE, LANE),
             vmem(ROADS * NPAR, 2 * LANE, dtype=BF16),
-            vmem(ROAD, 2 * LANE),
-            vmem(LANE, 2 * LANE),
+            vmem(ROAD * ROAD, 2 * LANE),
             vmem(72, LANE),
             vmem(3, 72, LANE),
             vmem(ROADS, LANE),

time: 81.1 us -> 65.8 us (0.81)
  Pallas kernels: 74.3 us -> 59 us
    pallas_call x1, Pallas kernels: 74.3 us -> 59 us  [on_device(): pl.pallas_call(kernel_all, out_shape=(jax.ShapeDtypeStruct((ROADS, LANE,...]
where the time goes in v4:
time: 65.8 us; the launch traced here: 65.6 us
  Pallas kernels  59 us (90%)
  local copies, waits for them, and re-layouts  5.93 us (9%)
  between operations  0.66 us (1%)
    pallas_call x1, Pallas kernels, on_device(): pl.pallas_call(kernel_all, out_shape=(jax.ShapeDtypeStruct((ROADS, LANE,...  59 us
    unnamed x7, local copies, waits for them, and re-layouts  5.93 us

profile of v4, /device:TPU:1, one launch (start us, length us, event | category | flops | bytes accessed | tf_op | source)
XLA Modules:
  0.0 65.6 jit_solution(16639145565727208481)
XLA Ops:
  0.6 59.0 %alignment.1 = (f32[64,128,128]{2,1,0:T(8,128)}, f32[8,512]{1,0:T(8,128)}, f32[8,512]{1,0:T(8,128)}) custom-call(f32[5,12,512]{2,1,0:T(8,128)} %ld.1, f32[12,8,512]{2,1,0:T(8,128)} %bitcast.7, f32[12,512]{1,0:T(8,128)} %me_ref.1, f32[12,512]{1,0:T(8,128)} %hw.1, s32[12,512]{1,0:T(8,128)} %hm.1, s32[1,512]{1,0:T(1,128)} %bitcast.11, s32[1,512]{1,0:T(1,128)} %bitcast.12, ...), custom_call_target="tpu_custom_call" | custom-call | tf_op jit(solution)/shard_map/alignment/pallas_call | solution.py:419
  59.7 0.0 copy-start.1
  59.7 0.0 copy-start
  59.7 4.7 %copy.15 = f32[64,128,128]{2,1,0:T(8,128)} copy(f32[64,128,128]{2,1,0:T(8,128)} %get-tuple-element.12) | data formatting | bytes 8388608
  64.4 0.0 copy-done.1
  64.4 0.6 copy.16
  65.0 0.0 copy-done
  65.0 0.6 copy.17
Async XLA Ops:
  59.7 4.7 %copy-start.1 = (f32[8,512]{1,0:T(8,128)S(1)}, f32[8,512]{1,0:T(8,128)}, u32[]{:S(2)}) copy-start(f32[8,512]{1,0:T(8,128)} %get-tuple-element.7) | copy-start | bytes 49156
  59.7 5.3 %copy-start = (f32[8,512]{1,0:T(8,128)S(1)}, f32[8,512]{1,0:T(8,128)}, u32[]{:S(2)}) copy-start(f32[8,512]{1,0:T(8,128)} %get-tuple-element.8) | copy-start | bytes 49156

commit v5 on v4

--- a/solution.py
+++ b/solution.py
@@ -176,16 +176,14 @@
         blocks[:, at, :] += (out[:, :LANE] + out[:, LANE:]).reshape(ROADS, NPAR, LANE)
 
 
-def symmetric(blocks):
-    def one(r, carry):
-        block = blocks[r]
-        blocks[r] = 0.5 * (block + block.T)
-        return carry
-
-    lax.fori_loop(0, ROADS, one, 0, unroll=4)
+def symmetric(blocks, r):
+    block = blocks[r]
+    blocks[r] = 0.5 * (block + block.T)
 
 
 HALF = 64
+LINES = 80
+OWN = slice(8, 72)
 
 
 def low_lanes(x):
@@ -198,15 +196,15 @@
     for d in range(1, NPAR):
         moved = jnp.where(off == float(d), pltpu.roll(wide, 8 * d, 1), moved)
     head, rest = moved[:, :LANE], moved[:, LANE:]
-    field[...] = jnp.zeros_like(field)
-    field[0:64, :] = low_lanes(head)
-    field[1:65, :] += low_lanes(pltpu.roll(head, HALF, 1))
-    field[2:66, :] += low_lanes(rest)
+    field[80:88, :] = jnp.zeros((8, LANE), F32)
+    field[0:80, :] = low_lanes(head)
+    field[1:81, :] += low_lanes(pltpu.roll(head, HALF, 1))
+    field[2:82, :] += low_lanes(rest)
 
 
 def gather(field, off):
-    head = field[0:64, :] + pltpu.roll(field[1:65, :], HALF, 1)
-    wide = jnp.concatenate([head, field[2:66, :]], axis=1)
+    head = field[0:80, :] + pltpu.roll(field[1:81, :], HALF, 1)
+    wide = jnp.concatenate([head, field[2:82, :]], axis=1)
     piece = jnp.where(off == 0.0, wide, 0.0)
     for d in range(1, NPAR):
         piece = jnp.where(off == float(d), pltpu.roll(wide, 2 * LANE - 8 * d, 1), piece)
@@ -244,10 +242,11 @@
     return (d // 8, lax.rem(d, 8))
 
 
-def kernel_all(ld, gd, me_ref, hw, hm, hc, tr, rs, pw, blocks_out, rhs_out, cor_out,
-               send, recv, lay, blocks, road_rhs, g_ref, t_ref, x_ref, hot_ref, mix_ref,
-               field, vec, mapped, prior, flat, up, down, from_prev, from_next, line, lines,
-               send_sem, recv_sem, rim_sem, line_sem, out_sem):
+def kernel_all(ld, gd, me_ref, hw, hm, hc, tr, rs, pw, blocks, rhs_out, cor_out,
+               send, recv, lay, road_rhs, g_ref, t_ref, x_ref, hot_ref, mix_ref,
+               part, vec, mapped, flat, info, info_prev, info_next, from_prev, from_next, blocks_prev, blocks_next,
+               line, lines,
+               send_sem, recv_sem, rim_sem, line_sem):
     trk, mod = position()
     me = trk * 8 + mod
     barrier = pltpu.get_barrier_semaphore()
@@ -282,7 +281,28 @@
         jnp.int32, (ROADS, ROADS), 1
     )
     off = jnp.sum(jnp.where(diagonal, start, 0.0), axis=1, keepdims=True)
-    prior[...] = to_rows(pw[...], flat)
+    nxt = place_of(lax.rem(me + 1, DEV))
+    prv = place_of(lax.rem(me + DEV - 1, DEV))
+
+    def to_next(source, target, n):
+        return pltpu.make_async_remote_copy(
+            source, target, rim_sem.at[n, 0], rim_sem.at[n, 1], device_id=nxt, device_id_type=MESH
+        )
+
+    def to_prev(source, target, n):
+        return pltpu.make_async_remote_copy(
+            source, target, rim_sem.at[n, 2], rim_sem.at[n, 3], device_id=prv, device_id_type=MESH
+        )
+
+    lanes = lax.broadcasted_iota(jnp.int32, (ROADS, LANE), 1)
+    info[...] = jnp.where(lanes == HALF, off, to_rows(pw[...], flat))
+    info_moves = (
+        to_next(info.at[56:64], info_prev, 0),
+        to_prev(info.at[0:8], info_next, 0),
+    )
+    for move in info_moves:
+        move.start()
+    mapped[...] = jnp.zeros_like(mapped)
     blocks[...] = jnp.zeros_like(blocks)
     road_rhs[...] = jnp.zeros_like(road_rhs)
 
@@ -294,52 +314,62 @@
 
     lax.fori_loop(0, DEV // GROUP, take_group, 0)
 
-    nxt = lax.rem(me + 1, DEV)
-    prv = lax.rem(me + DEV - 1, DEV)
-    out_copy = pltpu.make_async_copy(blocks, blocks_out, out_sem)
-
-    def exchange(e, target, between):
-        up[e] = field[64:72, :]
-        down[e] = field[0:8, :]
-        to_next = pltpu.make_async_remote_copy(
-            up.at[e], from_prev.at[e], rim_sem.at[e, 0], rim_sem.at[e, 1], device_id=place_of(nxt), device_id_type=MESH
-        )
-        to_prev = pltpu.make_async_remote_copy(
-            down.at[e], from_next.at[e], rim_sem.at[e, 2], rim_sem.at[e, 3], device_id=place_of(prv), device_id_type=MESH
-        )
-        to_next.start()
-        to_prev.start()
-        target[8:64, :] = field[8:64, :]
+    for move in info_moves:
+        move.wait()
+    edge = jnp.concatenate([info_prev[...], info[...], info_next[...]], axis=0)
+    prior = low_lanes(edge)
+    offs = edge[:, HALF : HALF + 1]
+
+    mapped[OWN, :] = road_rhs[...]
+    spread(mapped[...], offs, part)
+    rim_moves = (to_next(part.at[64:80], from_prev, 1), to_prev(part.at[8:16], from_next, 1))
+    for move in rim_moves:
+        move.start()
+    for r in (60, 61, 62, 63, 0, 1, 2, 3):
+        symmetric(blocks, r)
+    block_moves = (to_next(blocks.at[60:64], blocks_prev, 2), to_prev(blocks.at[0:2], blocks_next, 2))
+    for move in block_moves:
+        move.start()
+
+    def symmetric_four(k, carry):
+        for r in range(4):
+            symmetric(blocks, 4 * k + r)
+        return carry
+
+    lax.fori_loop(1, 15, symmetric_four, 0)
+    for move in rim_moves:
+        move.wait()
+    vec[0, 0:8, :] = from_prev[0:8, :]
+    vec[0, 8:16, :] = part[8:16, :] + from_prev[8:16, :]
+    vec[0, 16:72, :] = part[16:72, :]
+    vec[0, 72:80, :] = part[72:80, :] + from_next[...]
+    vec[0, 80:88, :] = jnp.zeros((8, LANE), F32)
+
+    def apply(source, target, between):
+        piece = gather(source, offs)
+        flipped = jnp.concatenate([piece, jnp.zeros((LANE - LINES, LANE), F32)], axis=0).T
+
+        def one(block, e):
+            mapped[e : e + 1, :] = jnp.sum(block * flipped[:, e : e + 1], axis=0, keepdims=True)
+
+        for r in range(ROADS):
+            one(blocks[r], r + 8)
         between()
-        to_next.wait()
-        to_prev.wait()
-        keep = lax.broadcasted_iota(jnp.int32, (8, LANE), 0) < 2
-        target[0:8, :] = field[0:8, :] + jnp.where(keep, from_prev[e], 0.0)
-        target[64:72, :] = jnp.where(keep, field[64:72, :] + from_next[e], 0.0)
-
-    def apply(source, e, target, between):
-        flipped = gather(source, off).T
-        for r in range(ROADS):
-            mapped[r : r + 1, :] = jnp.sum(blocks[r] * flipped[:, r : r + 1], axis=0, keepdims=True)
-        spread(mapped[...], off, field)
-        field[0:64, :] += prior[...] * source[0:64, :]
-        exchange(e, target, between)
-
-    def finish_blocks():
-        symmetric(blocks)
-        out_copy.start()
-
-    def give_rhs():
-        rhs_out[...] = from_rows(vec[0, 0:64, :], flat)
-
-    def nothing():
-        pass
-
-    spread(road_rhs[...], off, field)
-    exchange(0, vec.at[0], finish_blocks)
-    apply(vec.at[0], 1, vec.at[1], give_rhs)
-    apply(vec.at[1], 2, vec.at[2], nothing)
-    b, w, u = vec[0, 0:64, :], vec[1, 0:64, :], vec[2, 0:64, :]
+        for r in range(4):
+            one(blocks_prev[r], r + 4)
+        for r in range(2):
+            one(blocks_next[r], r + 72)
+        spread(mapped[...], offs, target)
+        target[0:80, :] += prior * source[0:80, :]
+
+    def take_blocks():
+        rhs_out[...] = from_rows(vec[0, OWN, :], flat)
+        for move in block_moves:
+            move.wait()
+
+    apply(vec.at[0], vec.at[1], take_blocks)
+    apply(vec.at[1], vec.at[2], lambda: None)
+    b, w, u = vec[0, OWN, :], vec[1, OWN, :], vec[2, OWN, :]
 
     def inverse(value):
         return jnp.where(value > 0.0, 1.0 / jnp.where(value > 0.0, value, 1.0), 0.0)
@@ -365,7 +395,7 @@
     w8 = from_rows(w, flat)
     whole = pltpu.make_async_remote_copy(
         lines.at[pl.ds(0, DEV - 1)], lines.at[pl.ds(0, DEV - 1)], line_sem.at[0], line_sem.at[1],
-        device_id=place_of(nxt), device_id_type=MESH,
+        device_id=nxt, device_id_type=MESH,
     )
     whole.wait_recv()
     for d in range(DEV):
@@ -403,10 +433,9 @@
     whole.wait_send()
     sent = pltpu.make_async_remote_copy(
         send.at[pl.ds(0, DEV - 1)], recv.at[pl.ds(0, DEV - 1)], send_sem, recv_sem.at[0],
-        device_id=place_of(nxt), device_id_type=MESH,
+        device_id=nxt, device_id_type=MESH,
     )
     sent.wait_send()
-    out_copy.wait()
 
 
 VM = pl.BlockSpec(memory_space=pltpu.VMEM)
@@ -424,38 +453,38 @@
             jax.ShapeDtypeStruct((NPAR, TRACKS), F32),
         ),
         in_specs=[VM] * 9,
-        out_specs=(pl.BlockSpec(memory_space=pl.ANY), VM, VM),
+        out_specs=(VM, VM, VM),
         scratch_shapes=[
             vmem(DEV, 24, LANE),
             vmem(DEV, 24, LANE),
             vmem(4, 192, LANE),
-            vmem(ROADS, LANE, LANE),
             vmem(ROADS, LANE),
             vmem(LANE, 2 * LANE),
             vmem(LANE, 2 * LANE),
             vmem(2, LANE, LANE),
             vmem(ROADS * NPAR, 2 * LANE, dtype=BF16),
             vmem(ROAD * ROAD, 2 * LANE),
-            vmem(72, LANE),
-            vmem(3, 72, LANE),
+            vmem(88, LANE),
+            vmem(3, 88, LANE),
+            vmem(LINES, LANE),
+            vmem(TRACKS, LANE),
             vmem(ROADS, LANE),
-            vmem(HALF, LANE),
-            vmem(TRACKS, LANE),
-            vmem(3, 8, LANE),
-            vmem(3, 8, LANE),
-            vmem(3, 8, LANE),
-            vmem(3, 8, LANE),
+            vmem(8, LANE),
+            vmem(8, LANE),
+            vmem(16, LANE),
+            vmem(8, LANE),
+            vmem(4, LANE, LANE),
+            vmem(2, LANE, LANE),
             vmem(1, LANE),
             vmem(DEV, 1, LANE),
             pltpu.SemaphoreType.DMA,
             pltpu.SemaphoreType.DMA((DEV // GROUP,)),
             pltpu.SemaphoreType.DMA((3, 4)),
             pltpu.SemaphoreType.DMA((2,)),
-            pltpu.SemaphoreType.DMA,
         ],
-        compiler_params=pltpu.CompilerParams(collective_id=0, has_side_effects=True),
+        compiler_params=pltpu.CompilerParams(collective_id=0, has_side_effects=True, vmem_limit_bytes=32 * 1024 * 1024),
         name="alignment",
-    )(
+    )(*(pltpu.with_memory_space_constraint(array, pltpu.HBM) for array in (
         ld,
         jnp.transpose(gd, (1, 0, 2)),
         me,
@@ -465,7 +494,7 @@
         tr.reshape(1, TRACKS),
         rs.reshape(1, ROADS),
         pw.T,
-    )
+    )))
     return blocks, rhs.T, cor.T
 
 

time: 65.8 us -> 54 us (0.82)
  Pallas kernels: 59 us -> 50 us
  local copies, waits for them, and re-layouts: 5.93 us -> 3.23 us
    pallas_call x1, Pallas kernels: 59 us -> 50 us  [on_device(): pl.pallas_call(kernel_all, out_shape=(jax.ShapeDtypeStruct((ROADS, LANE,...]
    unnamed x7 -> x3, local copies, waits for them, and re-layouts: 5.93 us -> 3.23 us
where the time goes in v5:
time: 54 us; the launch traced here: 53.8 us
  Pallas kernels  50 us (93%)
  local copies, waits for them, and re-layouts  3.23 us (6%)
  between operations  0.64 us (1%)
    pallas_call x1, Pallas kernels, on_device(): pl.pallas_call(kernel_all, out_shape=(jax.ShapeDtypeStruct((ROADS, LANE,...  50 us
    unnamed x3, local copies, waits for them, and re-layouts  3.23 us

profile of v5, /device:TPU:1, one launch (start us, length us, event | category | flops | bytes accessed | tf_op | source)
XLA Modules:
  0.0 53.8 jit_solution(6015055217345580284)
XLA Ops:
  0.6 50.0 %alignment.1 = (f32[64,128,128]{2,1,0:T(8,128)S(1)}, f32[8,512]{1,0:T(8,128)S(1)}, f32[8,512]{1,0:T(8,128)S(1)}) custom-call(f32[5,12,512]{2,1,0:T(8,128)} %ld.1, f32[12,8,512]{2,1,0:T(8,128)} %bitcast.9, f32[12,512]{1,0:T(8,128)} %me_ref.1, f32[12,512]{1,0:T(8,128)} %hw.1, s32[12,512]{1,0:T(8,128)} %hm.1, s32[1,512]{1,0:T(1,128)} %bitcast.11, ...), custom_call_target="tpu_custom_call" | custom-call | tf_op jit(solution)/shard_map/alignment/pallas_call | solution.py:448
  50.6 2.0 %copy.15 = f32[64,128,128]{2,1,0:T(8,128)} copy(f32[64,128,128]{2,1,0:T(8,128)S(1)} %get-tuple-element.12) | data formatting | bytes 8388608
  52.6 0.6 %copy.16 = f32[512,8]{0,1:T(8,128)} copy(f32[512,8]{0,1:T(8,128)S(1)} %bitcast.8) | data formatting | bytes 32768
  53.2 0.6 %copy.17 = f32[512,8]{0,1:T(8,128)} copy(f32[512,8]{0,1:T(8,128)S(1)} %bitcast.7) | data formatting | bytes 32768

commit v6 on v5

--- a/solution.py
+++ b/solution.py
@@ -242,7 +242,7 @@
     return (d // 8, lax.rem(d, 8))
 
 
-def kernel_all(ld, gd, me_ref, hw, hm, hc, tr, rs, pw, blocks, rhs_out, cor_out,
+def kernel_all(ld, gd, me_ref, hw, hm, hc, tr, rs, pw, blocks, pair,
                send, recv, lay, road_rhs, g_ref, t_ref, x_ref, hot_ref, mix_ref,
                part, vec, mapped, flat, info, info_prev, info_next, from_prev, from_next, blocks_prev, blocks_next,
                line, lines,
@@ -258,7 +258,11 @@
     cores = [core, 1 - core]
     trks = [zs[j // 4] + ys[j % 4] for j in range(GROUP)]
     mods = [xs[m // 2] + cores[m % 2] for m in range(8)]
-    others = [(trks[j], mods[m]) for m in range(8) for j in range(GROUP) if j or m]
+    step_cost = (0, 1, 2, 1)
+    far_first = sorted(
+        (-step_cost[j // 4] - step_cost[j % 4] - step_cost[m // 2], j, m) for m in range(8) for j in range(GROUP) if j or m
+    )
+    others = [(trks[j], mods[m]) for _, j, m in far_first]
     for other in others:
         pl.semaphore_signal(barrier, inc=1, device_id=other, device_id_type=MESH)
     own = pltpu.make_async_copy(send.at[0], recv.at[0], recv_sem.at[0])
@@ -363,7 +367,7 @@
         target[0:80, :] += prior * source[0:80, :]
 
     def take_blocks():
-        rhs_out[...] = from_rows(vec[0, OWN, :], flat)
+        pair[0:8, :] = from_rows(vec[0, OWN, :], flat)
         for move in block_moves:
             move.wait()
 
@@ -427,9 +431,9 @@
     determinant = first * second - cross * cross
     coef_one = beta_one * (second * alpha_one - cross * beta_two) / determinant
     coef_two = beta_one * (first * beta_two - cross * alpha_one) / determinant
-    v1 = rhs_out[...] * inv_one
+    v1 = pair[0:8, :] * inv_one
     v2 = (w8 * inv_one - alpha_one * v1) * inv_two
-    cor_out[...] = coef_one * v1 + coef_two * v2
+    pair[8:16, :] = coef_one * v1 + coef_two * v2
     whole.wait_send()
     sent = pltpu.make_async_remote_copy(
         send.at[pl.ds(0, DEV - 1)], recv.at[pl.ds(0, DEV - 1)], send_sem, recv_sem.at[0],
@@ -445,15 +449,14 @@
     def vmem(*shape, dtype=F32):
         return pltpu.VMEM(shape, dtype)
 
-    blocks, rhs, cor = pl.pallas_call(
+    blocks, pair = pl.pallas_call(
         kernel_all,
         out_shape=(
             jax.ShapeDtypeStruct((ROADS, LANE, LANE), F32),
-            jax.ShapeDtypeStruct((NPAR, TRACKS), F32),
-            jax.ShapeDtypeStruct((NPAR, TRACKS), F32),
+            jax.ShapeDtypeStruct((2 * NPAR, TRACKS), F32),
         ),
         in_specs=[VM] * 9,
-        out_specs=(VM, VM, VM),
+        out_specs=(VM, VM),
         scratch_shapes=[
             vmem(DEV, 24, LANE),
             vmem(DEV, 24, LANE),
@@ -495,7 +498,7 @@
         rs.reshape(1, ROADS),
         pw.T,
     )))
-    return blocks, rhs.T, cor.T
+    return blocks, pair[:NPAR].T, pair[NPAR:].T
 
 
 def solution(mesh):

time: 54 us -> 52.9 us (0.980)
  local copies, waits for them, and re-layouts: 3.23 us -> 2.63 us
    unnamed x3 -> x1, local copies, waits for them, and re-layouts: 3.23 us -> 2.01 us
    transpose x0 -> x1, local copies, waits for them, and re-layouts: none -> 0.61 us  [on_device(): return (blocks, pair[:NPAR].T, pair[NPAR:].T)]
where the time goes in v6:
time: 52.9 us; the launch traced here: 52.8 us
  Pallas kernels  49.5 us (94%)
  local copies, waits for them, and re-layouts  2.63 us (5%)
  between operations  0.64 us (1%)
    pallas_call x1, Pallas kernels, on_device(): pl.pallas_call(kernel_all, out_shape=(jax.ShapeDtypeStruct((ROADS, LANE,...  49.5 us
    unnamed x1, local copies, waits for them, and re-layouts  2.01 us

profile of v6, /device:TPU:1, one launch (start us, length us, event | category | flops | bytes accessed | tf_op | source)
XLA Modules:
  0.0 52.8 jit_solution(2804381061526406371)
XLA Ops:
  0.6 49.5 %alignment.1 = (f32[64,128,128]{2,1,0:T(8,128)S(1)}, f32[16,512]{1,0:T(8,128)S(1)}) custom-call(f32[5,12,512]{2,1,0:T(8,128)} %ld.1, f32[12,8,512]{2,1,0:T(8,128)} %bitcast.9, f32[12,512]{1,0:T(8,128)} %me_ref.1, f32[12,512]{1,0:T(8,128)} %hw.1, s32[12,512]{1,0:T(8,128)} %hm.1, s32[1,512]{1,0:T(1,128)} %bitcast.11, s32[1,512]{1,0:T(1,128)} %bitcast.12, ...), custom_call_target="tpu_custom_call" | custom-call | tf_op jit(solution)/shard_map/alignment/pallas_call | solution.py:452
  50.1 0.6 %slice_bitcast_fusion = (f32[512,8]{0,1:T(8,128)}, f32[512,8]{0,1:T(8,128)}) fusion(f32[16,512]{1,0:T(8,128)S(1)} %get-tuple-element.6), kind=kLoop, calls=%fused_computation | loop fusion | bytes 65536 | tf_op jit(solution)/shard_map/transpose | solution.py:501
  50.7 2.0 %copy.13 = f32[64,128,128]{2,1,0:T(8,128)} copy(f32[64,128,128]{2,1,0:T(8,128)S(1)} %get-tuple-element.12) | data formatting | bytes 8388608
